TPU v7x, 32 devices: a whole 2x2x4 slice. The times are simulated.
32 devices in a mesh: fsdp: 4 (over z), ctx: 2 (over y), tp: 4 (over x, core).
Axes of the slice: x: 2, y: 2, z: 4, core: 2. Of those that a mesh axis runs over, the one named last changes fastest.
Arguments:
- inputs: bfloat16 [12288, 768], P(('fsdp', 'ctx')), may hold values from -6 to 6
- segments: int32 [4, 3072], P('fsdp', 'ctx'), may hold values from 0 to 11, never falling along the last dimension, each value on 1 to 512 neighbouring positions
- w_query: bfloat16 [768, 768], P('fsdp', 'tp'), may hold values from -0.21875 to 0.21875
- b_query: bfloat16 [768], P('tp'), may hold values from -4 to 4
- w_key: bfloat16 [768, 768], P('fsdp', 'tp'), may hold values from -0.21875 to 0.21875
- w_value: bfloat16 [768, 768], P('fsdp', 'tp'), may hold values from -0.21875 to 0.21875
- b_value: bfloat16 [768], P('tp'), may hold values from -4 to 4
- w_out: bfloat16 [768, 768], P('tp', 'fsdp'), may hold values from -3 to 3
- b_out: bfloat16 [768], replicated, may hold values from -4 to 4
- gain_one: bfloat16 [768], replicated, may hold values from 0.099609375 to 1.8984375
- shift_one: bfloat16 [768], replicated, may hold values from -4 to 4
- w_inner: bfloat16 [768, 3072], P('fsdp', 'tp'), may hold values from -0.21875 to 0.21875
- b_inner: bfloat16 [3072], P('tp'), may hold values from -4 to 4
- w_outer: bfloat16 [3072, 768], P('tp', 'fsdp'), may hold values from -0.109375 to 0.109375
- b_outer: bfloat16 [768], replicated, may hold values from -4 to 4
- gain_two: bfloat16 [768], replicated, may hold values from 0.099609375 to 1.8984375
- shift_two: bfloat16 [768], replicated, may hold values from -4 to 4
- grad_output: bfloat16 [12288, 768], P(('fsdp', 'ctx')), may hold values from -6 to 6
Outputs:
- output: bfloat16 [12288, 768], P(('fsdp', 'ctx'))
- grad_inputs: float32 [12288, 768], P(('fsdp', 'ctx'))
- grad_w_query: float32 [768, 768], P('fsdp', 'tp')
- grad_b_query: float32 [768], P('tp')
- grad_w_key: float32 [768, 768], P('fsdp', 'tp')
- grad_w_value: float32 [768, 768], P('fsdp', 'tp')
- grad_b_value: float32 [768], P('tp')
- grad_w_out: float32 [768, 768], P('tp', 'fsdp')
- grad_b_out: float32 [768], replicated
- grad_gain_one: float32 [768], replicated
- grad_shift_one: float32 [768], replicated
- grad_w_inner: float32 [768, 3072], P('fsdp', 'tp')
- grad_b_inner: float32 [3072], P('tp')
- grad_w_outer: float32 [3072, 768], P('tp', 'fsdp')
- grad_b_outer: float32 [768], replicated
- grad_gain_two: float32 [768], replicated
- grad_shift_two: float32 [768], replicated
Inputs may be any that keep to these rules, and one draw needn't show every extreme that they name: `segments`: along each sequence the ids never fall and every id of 0 to 11 occurs; a document has 1 to 512 tokens, and one has exactly 512.
All inputs are finite; a program needn't handle non-finite values.
Results may differ from a plain program's by a relative error of at most 0.023.
Values may be sent and summed in bfloat16 or wider, within the bound.
No kernel may reach another device: no remote copies, remote signals or barrier semaphores. Data moves between devices by JAX's collectives and lax.ppermute only.
A program may use at most 128 MiB of HBM per device.

v0:
```python
import math

import jax
import jax.numpy as jnp
from jax import lax
from jax.sharding import PartitionSpec as P

HEAD_DIM = 64
MOST = 512


layer_eps = 1e-12
masked_score = -1e30


def padded(block, sides, width):
    for axis, dim in sides:
        count = lax.axis_size(axis)
        forward = [(i, i + 1) for i in range(count - 1)]
        backward = [(target, source) for source, target in forward]
        low = lax.ppermute(
            lax.slice_in_dim(block, block.shape[dim] - width, None, axis=dim), axis, forward
        )
        high = lax.ppermute(lax.slice_in_dim(block, 0, width, axis=dim), axis, backward)
        block = jnp.concatenate([low, block, high], axis=dim)
    return block


def product(left, right):
    return jnp.dot(left, right, preferred_element_type=jnp.float32)


def product_tn(left, right):
    return lax.dot_general(
        left, right, (((0,), (0,)), ((), ())), preferred_element_type=jnp.float32
    )


def product_nt(left, right):
    return lax.dot_general(
        left, right, (((1,), (1,)), ((), ())), preferred_element_type=jnp.float32
    )


def layer_norm(hidden, gain, shift):
    average = jnp.mean(hidden, axis=-1, keepdims=True)
    centred = hidden - average
    variance = jnp.mean(centred * centred, axis=-1, keepdims=True)
    return centred * lax.rsqrt(variance + layer_eps) * gain + shift


def gelu_exact(values):
    return 0.5 * values * (1.0 + jax.scipy.special.erf(values * 0.7071067811865476))


def correlations(seg_first, seg_second):
    return (jnp.max(seg_first) >= jnp.min(seg_second)) & (jnp.min(seg_first) <= jnp.max(seg_second))


def pair_grads(queries, grad_attn, lse_heads, delta_heads, seg_query, keys, values, seg_key, scale):
    scores = jnp.einsum("qhd,khd->hqk", queries, keys, preferred_element_type=jnp.float32) * scale
    same = seg_query[None, :, None] == seg_key[None, None, :]
    probs = jnp.where(same, jnp.exp(scores - lse_heads[:, :, None]), 0.0)
    grad_probs = jnp.einsum("qhd,khd->hqk", grad_attn, values, preferred_element_type=jnp.float32)
    grad_scores = (probs * (grad_probs - delta_heads[:, :, None])).astype(jnp.bfloat16)
    part_query = (
        jnp.einsum("hqk,khd->qhd", grad_scores, keys, preferred_element_type=jnp.float32) * scale
    )
    part_key = (
        jnp.einsum("hqk,qhd->khd", grad_scores, queries, preferred_element_type=jnp.float32) * scale
    )
    part_value = jnp.einsum(
        "hqk,qhd->khd", probs.astype(jnp.bfloat16), grad_attn, preferred_element_type=jnp.float32
    )
    return (part_query, part_key, part_value)


def add_rows(whole, first, width, part):
    current = lax.dynamic_slice_in_dim(whole, first, width, 0)
    return lax.dynamic_update_slice_in_dim(whole, current + part, first, 0)


def shards(
    inputs,
    segments,
    w_query,
    b_query,
    w_key,
    w_value,
    b_value,
    w_out,
    b_out,
    gain_one,
    shift_one,
    w_inner,
    b_inner,
    w_outer,
    b_outer,
    gain_two,
    shift_two,
    grad_output,
):
    rows = inputs.shape[0]
    width_model = inputs.shape[1]
    head_dim = HEAD_DIM
    local_width = w_query.shape[1]
    heads_local = local_width // head_dim
    scale = 1.0 / math.sqrt(head_dim)
    rim = MOST
    whole_query, whole_key, whole_value, whole_inner, whole_out, whole_outer = (
        lax.all_gather(w_query, "fsdp", axis=0, tiled=True),
        lax.all_gather(w_key, "fsdp", axis=0, tiled=True),
        lax.all_gather(w_value, "fsdp", axis=0, tiled=True),
        lax.all_gather(w_inner, "fsdp", axis=0, tiled=True),
        lax.all_gather(w_out, "fsdp", axis=1, tiled=True),
        lax.all_gather(w_outer, "fsdp", axis=1, tiled=True),
    )
    seg_rows = (segments.reshape(rows) + 1).astype(jnp.bfloat16)
    inputs_f = inputs.astype(jnp.float32)
    queries = (product(inputs, whole_query) + b_query.astype(jnp.float32)).astype(jnp.bfloat16)
    keys = product(inputs, whole_key).astype(jnp.bfloat16)
    values = (product(inputs, whole_value) + b_value.astype(jnp.float32)).astype(jnp.bfloat16)
    query_heads = queries.reshape(rows, heads_local, head_dim)
    ext_keys, ext_values, ext_seg = (
        padded(keys, (("ctx", 0),), rim),
        padded(values, (("ctx", 0),), rim),
        padded(seg_rows, (("ctx", 0),), rim),
    )
    ext_rows = ext_keys.shape[0]
    key_width = math.gcd(ext_rows, 512)
    key_blocks = ext_rows // key_width
    key_items = (
        ext_keys.reshape(key_blocks, key_width, heads_local, head_dim),
        ext_values.reshape(key_blocks, key_width, heads_local, head_dim),
        ext_seg.reshape(key_blocks, key_width),
        jnp.arange(key_blocks, dtype=jnp.int32),
    )

    def forward_visit(state, item):
        key_blk, value_blk, seg_blk, offset = item

        def forward_compute(kept):
            running, total, accum = kept
            scores = (
                jnp.einsum("qhd,khd->hqk", query_heads, key_blk, preferred_element_type=jnp.float32)
                * scale
            )
            same = seg_rows[None, :, None] == seg_blk[None, None, :]
            peak = jnp.maximum(running, jnp.max(jnp.where(same, scores, masked_score), axis=-1))
            factor = jnp.exp(running - peak)
            weights = jnp.where(same, jnp.exp(scores - peak[:, :, None]), 0.0)
            total = total * factor + jnp.sum(weights, axis=-1)
            accum = accum * factor.T[:, :, None] + jnp.einsum(
                "hqk,khd->qhd",
                weights.astype(jnp.bfloat16),
                value_blk,
                preferred_element_type=jnp.float32,
            )
            return (peak, total, accum)

        return (
            lax.cond(correlations(seg_rows, seg_blk), forward_compute, lambda kept: kept, state),
            None,
        )

    start_state = (
        jnp.full((heads_local, rows), masked_score, jnp.float32),
        jnp.zeros((heads_local, rows), jnp.float32),
        jnp.zeros((rows, heads_local, head_dim), jnp.float32),
    )
    (running, total, accum), _ = lax.scan(forward_visit, start_state, key_items)
    attended = accum / total.T[:, :, None]
    lse_heads = running + jnp.log(total)
    attended_low = attended.reshape(rows, local_width).astype(jnp.bfloat16)
    branch_part = product(attended_low, whole_out)
    gain_one_f = gain_one.astype(jnp.float32)
    shift_one_f = shift_one.astype(jnp.float32)
    gain_two_f = gain_two.astype(jnp.float32)
    shift_two_f = shift_two.astype(jnp.float32)
    branch = lax.psum(branch_part.astype(jnp.bfloat16), "tp").astype(jnp.float32) + b_out.astype(
        jnp.float32
    )
    normed_one, norm_one_back = jax.vjp(layer_norm, inputs_f + branch, gain_one_f, shift_one_f)
    normed_low = normed_one.astype(jnp.bfloat16)
    inner = product(normed_low, whole_inner) + b_inner.astype(jnp.float32)
    activ, gelu_back = jax.vjp(gelu_exact, inner)
    activ_low = activ.astype(jnp.bfloat16)
    outer = lax.psum(product(activ_low, whole_outer).astype(jnp.bfloat16), "tp").astype(
        jnp.float32
    ) + b_outer.astype(jnp.float32)
    result, norm_two_back = jax.vjp(layer_norm, normed_one + outer, gain_two_f, shift_two_f)
    output = result.astype(jnp.bfloat16)
    grad_hidden_two, grad_gain_two, grad_shift_two = norm_two_back(grad_output.astype(jnp.float32))
    grad_outer_low = grad_hidden_two.astype(jnp.bfloat16)
    grad_activ = product_nt(grad_outer_low, whole_outer)
    grad_inner_low = gelu_back(grad_activ)[0].astype(jnp.bfloat16)
    grad_normed = grad_hidden_two + lax.psum(
        product_nt(grad_inner_low, whole_inner).astype(jnp.bfloat16), "tp"
    ).astype(jnp.float32)
    grad_hidden_one, grad_gain_one, grad_shift_one = norm_one_back(grad_normed)
    grad_b_outer = jnp.sum(grad_outer_low.astype(jnp.float32), axis=0)
    grad_w_outer = product_tn(activ_low, grad_outer_low)
    grad_b_inner = jnp.sum(grad_inner_low.astype(jnp.float32), axis=0)
    grad_w_inner = product_tn(normed_low, grad_inner_low)
    grad_branch_low = grad_hidden_one.astype(jnp.bfloat16)
    grad_b_out = jnp.sum(grad_branch_low.astype(jnp.float32), axis=0)
    grad_w_out = product_tn(attended_low, grad_branch_low)
    grad_attn = product_nt(grad_branch_low, whole_out).astype(jnp.bfloat16)
    grad_attn_heads = grad_attn.reshape(rows, heads_local, head_dim)
    delta_heads = jnp.einsum("qhd,qhd->hq", grad_attn_heads.astype(jnp.float32), attended)

    def back_visit(state, item):
        key_blk, value_blk, seg_blk, offset = item

        def back_compute(kept):
            grad_q, grad_k, grad_v = kept
            part_query, part_key, part_value = pair_grads(
                query_heads,
                grad_attn_heads,
                lse_heads,
                delta_heads,
                seg_rows,
                key_blk,
                value_blk,
                seg_blk,
                scale,
            )
            first_key = offset * key_width
            return (
                grad_q + part_query,
                add_rows(grad_k, first_key, key_width, part_key),
                add_rows(grad_v, first_key, key_width, part_value),
            )

        return (
            lax.cond(correlations(seg_rows, seg_blk), back_compute, lambda kept: kept, state),
            None,
        )

    empty_ext = jnp.zeros((ext_rows, heads_local, head_dim), jnp.float32)
    (grad_q, grad_k_ext, grad_v_ext), _ = lax.scan(
        back_visit,
        (jnp.zeros((rows, heads_local, head_dim), jnp.float32), empty_ext, empty_ext),
        key_items,
    )
    grad_k_ext = grad_k_ext.reshape(ext_rows, local_width)
    grad_v_ext = grad_v_ext.reshape(ext_rows, local_width)
    send_keys = jnp.concatenate([grad_k_ext[:rim], grad_k_ext[rim + rows :]], axis=0)
    send_values = jnp.concatenate([grad_v_ext[:rim], grad_v_ext[rim + rows :]], axis=0)
    recv_keys, recv_values = (
        padded(send_keys.astype(jnp.bfloat16), (("ctx", 0),), rim).astype(send_keys.dtype),
        padded(send_values.astype(jnp.bfloat16), (("ctx", 0),), rim).astype(send_values.dtype),
    )
    grad_k = grad_k_ext[rim : rim + rows]
    grad_k = grad_k.at[:rim].add(recv_keys[:rim]).at[rows - rim :].add(recv_keys[3 * rim :])
    grad_v = grad_v_ext[rim : rim + rows]
    grad_v = grad_v.at[:rim].add(recv_values[:rim]).at[rows - rim :].add(recv_values[3 * rim :])
    grad_q_low = grad_q.reshape(rows, local_width).astype(jnp.bfloat16)
    grad_k_low = grad_k.astype(jnp.bfloat16)
    grad_v_low = grad_v.astype(jnp.bfloat16)
    grad_b_query = jnp.sum(grad_q_low.astype(jnp.float32), axis=0)
    grad_b_value = jnp.sum(grad_v_low.astype(jnp.float32), axis=0)
    grad_w_query = product_tn(inputs, grad_q_low)
    grad_w_key = product_tn(inputs, grad_k_low)
    grad_w_value = product_tn(inputs, grad_v_low)
    grad_input_part = (
        product_nt(grad_q_low, whole_query)
        + product_nt(grad_k_low, whole_key)
        + product_nt(grad_v_low, whole_value)
    )
    grad_inputs = grad_hidden_one + lax.psum(grad_input_part.astype(jnp.bfloat16), "tp").astype(
        jnp.float32
    )
    totals = lax.psum(
        (
            grad_w_query,
            grad_w_key,
            grad_w_value,
            grad_w_inner,
            grad_w_out,
            grad_w_outer,
            grad_b_query,
            grad_b_value,
            grad_b_out,
            grad_gain_one,
            grad_shift_one,
            grad_b_inner,
            grad_b_outer,
            grad_gain_two,
            grad_shift_two,
        ),
        ("fsdp", "ctx"),
    )
    owner = lax.axis_index("fsdp")
    piece = width_model // lax.axis_size("fsdp")
    first_row = owner * piece
    shard_query = lax.dynamic_slice_in_dim(totals[0], first_row, piece, 0)
    shard_key = lax.dynamic_slice_in_dim(totals[1], first_row, piece, 0)
    shard_value = lax.dynamic_slice_in_dim(totals[2], first_row, piece, 0)
    shard_inner = lax.dynamic_slice_in_dim(totals[3], first_row, piece, 0)
    shard_out = lax.dynamic_slice_in_dim(totals[4], first_row, piece, 1)
    shard_outer = lax.dynamic_slice_in_dim(totals[5], first_row, piece, 1)
    small = totals[6:]
    return (
        output,
        grad_inputs,
        shard_query,
        small[0],
        shard_key,
        shard_value,
        small[1],
        shard_out,
        small[2],
        small[3],
        small[4],
        shard_inner,
        small[5],
        shard_outer,
        small[6],
        small[7],
        small[8],
    )


def solution(mesh):
    return jax.shard_map(
        shards,
        mesh=mesh,
        in_specs=(
            P(("fsdp", "ctx"), None),
            P("fsdp", "ctx"),
            P("fsdp", "tp"),
            P("tp"),
            P("fsdp", "tp"),
            P("fsdp", "tp"),
            P("tp"),
            P("tp", "fsdp"),
            P(),
            P(),
            P(),
            P("fsdp", "tp"),
            P("tp"),
            P("tp", "fsdp"),
            P(),
            P(),
            P(),
            P(("fsdp", "ctx"), None),
        ),
        out_specs=(
            P(("fsdp", "ctx"), None),
            P(("fsdp", "ctx"), None),
            P("fsdp", "tp"),
            P("tp"),
            P("fsdp", "tp"),
            P("fsdp", "tp"),
            P("tp"),
            P("tp", "fsdp"),
            P(),
            P(),
            P(),
            P("fsdp", "tp"),
            P("tp"),
            P("tp", "fsdp"),
            P(),
            P(),
            P(),
        ),
        check_vma=False,
    )
```

profile of v0, /device:TPU:10, one launch (start us, length us, event | category | flops | bytes accessed | tf_op | source)
XLA Modules:
  0.0 829.9 jit_solution(6891239765329887523)
XLA Ops:
  9.5 3.4 collective-permute-start
  14.9 15.5 %all_gather.20 = bf16[768,192]{1,0:T(8,128)(2,1)S(1)} all-gather(bf16[192,192]{1,0:T(8,128)(2,1)} %param.39), channel_id=1, replica_groups=mesh['fsdp'=4,'ctx'=2,'tp'=4] {'fsdp'}, dimensions={0}, use_global_device_ids=true | all-gather | bytes 368640 | tf_op jit(solution)/shard_map/all_gather | solution.py:113
  30.5 2.7 fusion.65
  34.2 5.5 collective-permute-start.4
  39.6 15.1 %all_gather.18 = bf16[768,192]{1,0:T(8,128)(2,1)S(1)} all-gather(bf16[192,192]{1,0:T(8,128)(2,1)S(1)} %copy-done.34), channel_id=1, replica_groups=mesh['fsdp'=4,'ctx'=2,'tp'=4] {'fsdp'}, dimensions={0}, use_global_device_ids=true | all-gather | bytes 368640 | tf_op jit(solution)/shard_map/all_gather | solution.py:112
  62.0 14.7 %all_gather.19 = bf16[768,192]{1,0:T(8,128)(2,1)S(1)} all-gather(bf16[192,192]{1,0:T(8,128)(2,1)} %param.36), channel_id=1, replica_groups=mesh['fsdp'=4,'ctx'=2,'tp'=4] {'fsdp'}, dimensions={0}, use_global_device_ids=true | all-gather | bytes 368640 | tf_op jit(solution)/shard_map/all_gather | solution.py:111
  78.5 15.3 %all_gather.21 = bf16[192,768]{0,1:T(8,128)(2,1)} all-gather(bf16[192,192]{0,1:T(8,128)(2,1)} %copy.63), channel_id=1, replica_groups=mesh['fsdp'=4,'ctx'=2,'tp'=4] {'fsdp'}, dimensions={1}, use_global_device_ids=true | all-gather | bytes 368640 | tf_op jit(solution)/shard_map/all_gather | solution.py:115
  99.3 3.6 reshape.324
  102.9 2.7 copy.61
  107.6 3.5 reshape.326
  111.1 2.7 copy.62
  115.0 56.0 %while.35 = (s32[]{:T(128)}, f32[3,1536]{1,0:T(4,128)S(1)}, f32[3,1536]{1,0:T(4,128)S(1)}, f32[1536,3,64]{0,2,1:T(8,128)}, bf16[5,512]{1,0:T(8,128)(2,1)S(1)}, /...) while((s32[]{:T(128)}, f32[3,1536]{1,0:T(4,128)S(1)}, ...), condition=%wide.region_9.10_spmd, body=%wide.region_2.9_spmd.sunk | while | flops 631323136 | bytes 44541264 | solution.py:171
  121.4 10.0 %conditional.5 = ((f32[3,1536]{1,0:T(4,128)S(1)}, f32[3,1536]{1,0:T(4,128)S(1)}, f32[1536,3,64]{0,2,1:T(8,128)})) conditional(s32[]{:T(128)} %convert_element_type.353, (f32[3,1536]{1,0:T(4,128)S(1)}, f32[3,1536]{1,0:T(4,128)S(1)}, f32[1536,3,64]{0,2,1:T(8,128)}) %tuple.128, (bf16[1536]{0:T(1024)(128)(2,1)S(1)}, bf16[1,512]{1,0:T(2,128)(2,1)S(1)}, ...), branch_computations={%region_5.5_spmd, %region_6.8_spmd} | conditional | flops 631322112 | bytes 44538972 | solution.py:162
  121.9 2.9 fusion.2
  126.9 3.4 fusion.13
  134.6 10.0 %conditional.5 = ((f32[3,1536]{1,0:T(4,128)S(1)}, f32[3,1536]{1,0:T(4,128)S(1)}, f32[1536,3,64]{0,2,1:T(8,128)})) conditional(s32[]{:T(128)} %convert_element_type.353, (f32[3,1536]{1,0:T(4,128)S(1)}, f32[3,1536]{1,0:T(4,128)S(1)}, f32[1536,3,64]{0,2,1:T(8,128)}) %tuple.128, (bf16[1536]{0:T(1024)(128)(2,1)S(1)}, bf16[1,512]{1,0:T(2,128)(2,1)S(1)}, ...), branch_computations={%region_5.5_spmd, %region_6.8_spmd} | conditional | flops 631322112 | bytes 44538972 | solution.py:162
  135.1 2.9 fusion.2
  140.1 3.4 fusion.13
  147.8 10.0 %conditional.5 = ((f32[3,1536]{1,0:T(4,128)S(1)}, f32[3,1536]{1,0:T(4,128)S(1)}, f32[1536,3,64]{0,2,1:T(8,128)})) conditional(s32[]{:T(128)} %convert_element_type.353, (f32[3,1536]{1,0:T(4,128)S(1)}, f32[3,1536]{1,0:T(4,128)S(1)}, f32[1536,3,64]{0,2,1:T(8,128)}) %tuple.128, (bf16[1536]{0:T(1024)(128)(2,1)S(1)}, bf16[1,512]{1,0:T(2,128)(2,1)S(1)}, ...), branch_computations={%region_5.5_spmd, %region_6.8_spmd} | conditional | flops 631322112 | bytes 44538972 | solution.py:162
  148.3 2.9 fusion.2
  153.3 3.4 fusion.13
  161.0 10.0 %conditional.5 = ((f32[3,1536]{1,0:T(4,128)S(1)}, f32[3,1536]{1,0:T(4,128)S(1)}, f32[1536,3,64]{0,2,1:T(8,128)})) conditional(s32[]{:T(128)} %convert_element_type.353, (f32[3,1536]{1,0:T(4,128)S(1)}, f32[3,1536]{1,0:T(4,128)S(1)}, f32[1536,3,64]{0,2,1:T(8,128)}) %tuple.128, (bf16[1536]{0:T(1024)(128)(2,1)S(1)}, bf16[1,512]{1,0:T(2,128)(2,1)S(1)}, ...), branch_computations={%region_5.5_spmd, %region_6.8_spmd} | conditional | flops 631322112 | bytes 44538972 | solution.py:162
  161.5 2.9 fusion.2
  166.5 3.4 fusion.13
  177.3 56.7 %all-reduce.8.cloned.1.call-done = bf16[1536,768]{1,0:T(8,128)(2,1)} async-done(((bf16[1536,768]{1,0:T(8,128)(2,1)}), bf16[1536,768]{1,0:T(8,128)(2,1)}) %all-reduce.8.cloned.1.call-update) | async-done | bytes 2359312 | tf_op jit(solution)/shard_map/psum | solution.py:180
  234.0 2.7 fusion.62
  238.0 7.0 multiply_convert_fusion
  245.0 5.5 convolution_convert_fusion.1
  251.2 55.2 %all-reduce.10.cloned.1.call-done = bf16[1536,768]{1,0:T(8,128)(2,1)} async-done(((bf16[1536,768]{1,0:T(8,128)(2,1)}), bf16[1536,768]{1,0:T(8,128)(2,1)}) %all-reduce.10.cloned.1.call-update) | async-done | bytes 2359312 | tf_op jit(solution)/shard_map/psum | solution.py:188
  306.4 4.0 fusion.93
  312.1 2.8 fusion.60
  315.0 3.5 fusion.92
  320.6 5.4 convert_reduce_fusion.2
  327.3 3.5 convolution_convert_fusion
  330.9 6.0 fusion.100
  336.9 4.3 fusion.82
  341.2 45.5 %all-reduce.12.cloned.1.call-done = bf16[1536,768]{1,0:T(8,128)(2,1)} async-done(((bf16[1536,768]{1,0:T(8,128)(2,1)}), bf16[1536,768]{1,0:T(8,128)(2,1)}) %all-reduce.12.cloned.1.call-update) | async-done | bytes 2359312 | tf_op jit(solution)/shard_map/psum | solution.py:197
  386.7 7.2 multiply_reduce_fusion
  394.0 4.8 fusion.91
  406.0 88.0 %while.36 = (s32[]{:T(128)}, f32[1536,3,64]{0,2,1:T(8,128)}, f32[2560,3,64]{0,2,1:T(8,128)}, f32[2560,3,64]{0,2,1:T(8,128)}, bf16[5,512]{1,0:T(8,128)(2,1)S(1)},...) while((s32[]{:T(128)}, f32[1536,3,64]{0,2,1:T(8,128)}, ...), condition=%wide.region_26.27_spmd.clone, body=%wide.region_21.26_spmd.clone.sunk | while | flops 1535214592 | bytes 63717424 | solution.py:241
  412.2 18.2 %conditional.6 = ((f32[1536,3,64]{0,2,1:T(8,128)}, f32[2560,3,64]{0,2,1:T(8,128)}, f32[2560,3,64]{0,2,1:T(8,128)})) conditional(s32[]{:T(128)} %convert_element_type.354, (f32[1536,3,64]{0,2,1:T(8,128)}, f32[2560,3,64]{0,2,1:T(8,128)}, f32[2560,3,64]{0,2,1:T(8,128)}) %tuple.132, (bf16[1536]{0:T(1024)(128)(2,1)S(1)}, bf16[1,512]{1,0:T(2,128)(2,1)S(1)}, ...), branch_computations={%region_24.24_spmd, %region_25.25_spmd} | conditional | flops 1535213568 | bytes 63715052 | solution.py:236
  416.3 3.9 fusion.42
  420.2 4.5 fusion.26
  426.7 3.7 fusion.38
  433.4 18.1 %conditional.6 = ((f32[1536,3,64]{0,2,1:T(8,128)}, f32[2560,3,64]{0,2,1:T(8,128)}, f32[2560,3,64]{0,2,1:T(8,128)})) conditional(s32[]{:T(128)} %convert_element_type.354, (f32[1536,3,64]{0,2,1:T(8,128)}, f32[2560,3,64]{0,2,1:T(8,128)}, f32[2560,3,64]{0,2,1:T(8,128)}) %tuple.132, (bf16[1536]{0:T(1024)(128)(2,1)S(1)}, bf16[1,512]{1,0:T(2,128)(2,1)S(1)}, ...), branch_computations={%region_24.24_spmd, %region_25.25_spmd} | conditional | flops 1535213568 | bytes 63715052 | solution.py:236
  437.6 3.9 fusion.42
  441.5 4.5 fusion.26
  447.9 3.6 fusion.38
  454.6 18.1 %conditional.6 = ((f32[1536,3,64]{0,2,1:T(8,128)}, f32[2560,3,64]{0,2,1:T(8,128)}, f32[2560,3,64]{0,2,1:T(8,128)})) conditional(s32[]{:T(128)} %convert_element_type.354, (f32[1536,3,64]{0,2,1:T(8,128)}, f32[2560,3,64]{0,2,1:T(8,128)}, f32[2560,3,64]{0,2,1:T(8,128)}) %tuple.132, (bf16[1536]{0:T(1024)(128)(2,1)S(1)}, bf16[1,512]{1,0:T(2,128)(2,1)S(1)}, ...), branch_computations={%region_24.24_spmd, %region_25.25_spmd} | conditional | flops 1535213568 | bytes 63715052 | solution.py:236
  458.8 3.9 fusion.42
  462.7 4.5 fusion.26
  469.1 3.6 fusion.38
  475.8 18.1 %conditional.6 = ((f32[1536,3,64]{0,2,1:T(8,128)}, f32[2560,3,64]{0,2,1:T(8,128)}, f32[2560,3,64]{0,2,1:T(8,128)})) conditional(s32[]{:T(128)} %convert_element_type.354, (f32[1536,3,64]{0,2,1:T(8,128)}, f32[2560,3,64]{0,2,1:T(8,128)}, f32[2560,3,64]{0,2,1:T(8,128)}) %tuple.132, (bf16[1536]{0:T(1024)(128)(2,1)S(1)}, bf16[1,512]{1,0:T(2,128)(2,1)S(1)}, ...), branch_computations={%region_24.24_spmd, %region_25.25_spmd} | conditional | flops 1535213568 | bytes 63715052 | solution.py:236
  480.0 3.9 fusion.42
  483.9 4.5 fusion.26
  490.3 3.6 fusion.38
  500.0 4.7 collective-permute-start.8
  506.0 4.8 collective-permute-start.6
  518.5 3.1 fusion.99
  523.1 2.7 convolution_bitcast_fusion
  528.7 36.0 %all-reduce = (f32[192]{0:T(256)}, f32[192]{0:T(256)}, f32[768]{0:T(1024)}, f32[768]{0:T(1024)}, f32[768]{0:T(1024)}, /*index=5*/f32[768]{0:T(1024)}, f32[768]{0:T(1024)}, f32[768]{0:T(1024)}, f32[768]{0:T(1024)}) all-reduce(f32[192]{0:T(256)S(1)} %reduce_sum.182, ...), channel_id=1, replica_groups=mesh['fsdp'=4,'ctx'=2,'tp'=4] {'fsdp','ctx'}, use_global_device_ids=true, to_apply=%region_30.31 | all-reduce | flops 5760 | bytes 46080 | tf_op jit(solution)/shard_map/psum | solution.py:274
  564.7 10.6 %all-reduce.14.cloned.1.call-done = bf16[1536,768]{1,0:T(8,128)(2,1)} async-done(((bf16[1536,768]{1,0:T(8,128)(2,1)}), bf16[1536,768]{1,0:T(8,128)(2,1)}) %all-reduce.14.cloned.1.call-update) | async-done | bytes 2359312 | tf_op jit(solution)/shard_map/psum | solution.py:271
  575.4 5.8 convert_add_fusion
  581.1 231.2 %all-reduce.16.cloned.1.call-done = (f32[768,192]{0,1:T(8,128)}, f32[768,192]{0,1:T(8,128)}, f32[768,192]{0,1:T(8,128)}, f32[192,768]{1,0:T(8,128)}, f32[768,768]{1,0:T(8,128)}, /*index=5*/f32[768,768]{0,1:T(8,128)}) async-done(((f32[768,192]{0,1:T(8,128)}, f32[768,192]{0,1:T(8,128)}, f32[768,192]{0,1:T(8,128)}, f32[192,768]{1,0:T(8,128)}, f32[768,768]{1,0:T(8,128)}, /*index=5*/f32[768,768]{0,1:T(8,128)}), ...) | async-done | bytes 7077904 | tf_op jit(solution)/shard_map/psum | solution.py:274
  (330 shorter events, 114.5 us)
Async XLA Ops:
  8.0 51.7 %copy-start.38 = (s32[1,1536]{1,0:T(1,128)S(1)}, s32[1,1536]{1,0:T(1,128)}, u32[]{:S(2)}) copy-start(s32[1,1536]{1,0:T(1,128)} %param.35) | copy-start | bytes 18436
  8.0 46.7 %copy-start = (bf16[1536,768]{1,0:T(8,128)(2,1)S(1)}, bf16[1536,768]{1,0:T(8,128)(2,1)}, u32[]{:S(2)}) copy-start(bf16[1536,768]{1,0:T(8,128)(2,1)} %param.34) | copy-start | bytes 7077892
  8.0 31.6 %copy-start.34 = (bf16[192,192]{1,0:T(8,128)(2,1)S(1)}, bf16[192,192]{1,0:T(8,128)(2,1)}, u32[]{:S(2)}) copy-start(bf16[192,192]{1,0:T(8,128)(2,1)} %param.38) | copy-start | bytes 221188
  8.1 225.9 %all-reduce.8.cloned.1.call-start = ((), (), s32[]{:S(2)}) async-start(), calls=%async_computation | async-start | bytes 4718592 | tf_op jit(solution)/shard_map/psum | solution.py:180
  8.1 52.3 %copy-start.56 = (bf16[192]{0:T(256)(128)(2,1)S(1)}, bf16[192]{0:T(256)(128)(2,1)}, u32[]{:S(2)}) copy-start(bf16[192]{0:T(256)(128)(2,1)} %param.37) | copy-start | bytes 1156
  9.5 84.3 %collective-permute-start = (bf16[512]{0:T(512)(128)(2,1)}, bf16[512]{0:T(512)(128)(2,1)S(1)}, u32[]{:S(2)}, u32[]{:S(2)}) collective-permute-start(bf16[512]{0:T(512)(128)(2,1)} %get-tuple-element.665), channel_id=1, source_target_pairs={{0,4},{1,5},{2,6},{3,7},{8,12},{9,13},{10,14},{11,15},{16,20},{17,... | collective-permute-start | bytes 3080 | tf_op jit(solution)/shard_map/ppermute | solution.py:21
  13.0 82.3 %collective-permute-start.1 = (bf16[512]{0:T(512)(128)(2,1)}, bf16[512]{0:T(512)(128)(2,1)}, u32[]{:S(2)}, u32[]{:S(2)}) collective-permute-start(bf16[512]{0:T(512)(128)(2,1)} %get-tuple-element.666), channel_id=1, source_target_pairs={{4,0},{5,1},{6,2},{7,3},{12,8},{13,9},{14,10},{15,11},{20,16},{21,... | collective-permute-start | bytes 3080 | tf_op jit(solution)/shard_map/ppermute | solution.py:24
  30.5 9.2 %copy-start.30 = (bf16[768,192]{1,0:T(8,128)(2,1)}, bf16[768,192]{1,0:T(8,128)(2,1)S(1)}, u32[]{:S(2)}) copy-start(bf16[768,192]{1,0:T(8,128)(2,1)S(1)} %all_gather.20) | copy-start | bytes 884740
  34.2 71.4 %collective-permute-start.4 = (bf16[512,192]{0,1:T(8,128)(2,1)}, bf16[512,192]{0,1:T(8,128)(2,1)}, u32[]{:S(2)}, u32[]{:S(2)}) collective-permute-start(bf16[512,192]{0,1:T(8,128)(2,1)} %get-tuple-element.757), channel_id=1, source_target_pairs={{0,4},{1,5},{2,6},{3,7},{8,12},{9,13},{10,14},{11,15},{16,20},{17,... | collective-permute-start | bytes 589832 | tf_op jit(solution)/shard_map/ppermute | solution.py:21
  54.7 7.3 copy-start.20
  56.4 40.8 %collective-permute-start.2 = (bf16[512,192]{0,1:T(8,128)(2,1)}, bf16[512,192]{0,1:T(8,128)(2,1)}, u32[]{:S(2)}, u32[]{:S(2)}) collective-permute-start(bf16[512,192]{0,1:T(8,128)(2,1)} %get-tuple-element.759), channel_id=1, source_target_pairs={{0,4},{1,5},{2,6},{3,7},{8,12},{9,13},{10,14},{11,15},{16,20},{17,... | collective-permute-start | bytes 589832 | tf_op jit(solution)/shard_map/ppermute | solution.py:21
  58.4 38.9 %collective-permute-start.3 = (bf16[512,192]{0,1:T(8,128)(2,1)}, bf16[512,192]{0,1:T(8,128)(2,1)}, u32[]{:S(2)}, u32[]{:S(2)}) collective-permute-start(bf16[512,192]{0,1:T(8,128)(2,1)} %get-tuple-element.760), channel_id=1, source_target_pairs={{4,0},{5,1},{6,2},{7,3},{12,8},{13,9},{14,10},{15,11},{20,16},{21,... | collective-permute-start | bytes 589832 | tf_op jit(solution)/shard_map/ppermute | solution.py:24
  93.8 11.8 %collective-permute-start.5 = (bf16[512,192]{0,1:T(8,128)(2,1)}, bf16[512,192]{0,1:T(8,128)(2,1)}, u32[]{:S(2)}, u32[]{:S(2)}) collective-permute-start(bf16[512,192]{0,1:T(8,128)(2,1)} %get-tuple-element.758), channel_id=1, source_target_pairs={{4,0},{5,1},{6,2},{7,3},{12,8},{13,9},{14,10},{15,11},{20,16},{21,... | collective-permute-start | bytes 589832 | tf_op jit(solution)/shard_map/ppermute | solution.py:24
  99.3 6.3 copy-start.29
  115.0 58.2 %copy-start.22 = (bf16[192,768]{0,1:T(8,128)(2,1)S(1)}, bf16[192,768]{0,1:T(8,128)(2,1)}, u32[]{:S(2)}) copy-start(bf16[192,768]{0,1:T(8,128)(2,1)} %all_gather.21) | copy-start | bytes 884740
  171.0 6.2 copy-start.47
  171.0 6.2 copy-start.48
  171.0 6.2 copy-start.49
  171.0 6.2 copy-start.50
  175.5 62.5 %all-gather.3.cloned.1.call-start = ((), (), s32[]{:S(2)}) async-start(), calls=%async_computation.1 | async-start | bytes 1474560 | tf_op jit(solution)/shard_map/all_gather | solution.py:114
  176.1 68.9 %all-gather.5.cloned.1.call-start = ((), (), s32[]{:S(2)}) async-start(), calls=%async_computation.2 | async-start | bytes 1474560 | tf_op jit(solution)/shard_map/all_gather | solution.py:116
  176.7 129.7 %all-reduce.10.cloned.1.call-start = ((), (), s32[]{:S(2)}) async-start(), calls=%async_computation.3 | async-start | bytes 4718592 | tf_op jit(solution)/shard_map/psum | solution.py:188
  234.0 2.7 copy-start.2
  245.0 5.6 copy-start.51
  245.0 5.6 copy-start.52
  245.0 5.6 copy-start.53
  250.5 136.2 %all-reduce.12.cloned.1.call-start = ((), (), s32[]{:S(2)}) async-start(), calls=%async_computation.4 | async-start | bytes 4718592 | tf_op jit(solution)/shard_map/psum | solution.py:197
  314.9 4.6 slice-start
  314.9 4.6 slice-start.1
  318.4 7.5 copy-start.1
  319.5 6.4 copy-start.27
  320.6 6.8 copy-start.54
  330.8 244.5 %all-reduce.14.cloned.1.call-start = ((), (), s32[]{:S(2)}) async-start(), calls=%async_computation.5 | async-start | bytes 4718592 | tf_op jit(solution)/shard_map/psum | solution.py:271
  330.9 6.0 copy-start.3
  330.9 6.0 copy-start.58
  386.7 7.2 copy-start.4
  386.7 7.3 copy-start.17
  399.9 6.1 copy-start.19
  401.0 5.0 copy-start.25
  413.9 2.4 copy-start.26
  416.3 3.9 copy-start.37
  420.2 4.5 copy-start.5
  426.6 3.7 copy-start.6
  435.1 2.4 copy-start.26
  437.5 3.9 copy-start.37
  441.5 4.5 copy-start.5
  447.9 3.7 copy-start.6
  458.7 3.9 copy-start.37
  462.7 4.5 copy-start.5
  469.1 3.6 copy-start.6
  477.5 2.4 copy-start.26
  479.9 3.9 copy-start.37
  483.9 4.5 copy-start.5
  490.3 3.6 copy-start.6
  493.9 4.3 copy-start.9
  498.2 12.6 %copy-start.33 = (bf16[768,192]{1,0:T(8,128)(2,1)S(1)}, bf16[768,192]{1,0:T(8,128)(2,1)}, u32[]{:S(2)}) copy-start(bf16[768,192]{1,0:T(8,128)(2,1)} %copy-done.32) | copy-start | bytes 884740
  498.7 16.2 %collective-permute-start.9 = (bf16[512,192]{0,1:T(8,128)(2,1)S(1)}, bf16[512,192]{0,1:T(8,128)(2,1)S(1)}, u32[]{:S(2)}, u32[]{:S(2)}) collective-permute-start(bf16[512,192]{0,1:T(8,128)(2,1)S(1)} %bitcast.152), channel_id=1, source_target_pairs={{4,0},{5,1},{6,2},{7,3},{12,8},{13,9},{14,10},{15,11},{20,16},{21,... | collective-permute-start | bytes 589832 | tf_op jit(solution)/shard_map/ppermute | solution.py:24
  500.0 14.0 %copy-start.21 = (bf16[768,192]{1,0:T(8,128)(2,1)S(1)}, bf16[768,192]{1,0:T(8,128)(2,1)}, u32[]{:S(2)}) copy-start(bf16[768,192]{1,0:T(8,128)(2,1)} %copy-done.20) | copy-start | bytes 884740
  500.0 14.9 %collective-permute-start.8 = (bf16[512,192]{0,1:T(8,128)(2,1)S(1)}, bf16[512,192]{0,1:T(8,128)(2,1)S(1)}, u32[]{:S(2)}, u32[]{:S(2)}) collective-permute-start(bf16[512,192]{0,1:T(8,128)(2,1)S(1)} %bitcast.149), channel_id=1, source_target_pairs={{0,4},{1,5},{2,6},{3,7},{8,12},{9,13},{10,14},{11,15},{16,20},{17,... | collective-permute-start | bytes 589832 | tf_op jit(solution)/shard_map/ppermute | solution.py:21
  504.7 7.9 collective-permute-start.7
  506.0 7.8 collective-permute-start.6
  518.5 293.9 %all-reduce.16.cloned.1.call-start = ((), (), s32[]{:S(2)}) async-start(), calls=%async_computation.6 | async-start | bytes 14155776 | tf_op jit(solution)/shard_map/psum | solution.py:274
  521.6 4.2 copy-start.13
  527.3 48.0 %copy-start.36 = (f32[1536]{0:T(1024)S(1)}, f32[1536]{0:T(1024)}, u32[]{:S(2)}) copy-start(f32[1536]{0:T(1024)} %copy-done.35) | copy-start | bytes 18436
  (35 other events, 58.4 us)
Sparse Core Ops, SparseCore 0:
  175.7 58.2 all-reduce.7
  250.6 55.7 all-reduce.9
  330.9 55.7 all-reduce.11
  518.6 56.7 all-reduce.13
  580.9 231.4 all-reduce.15
Sparse Core Ops, SparseCore 1:
  177.6 33.4 all-gather.2
  212.4 29.3 all-gather.4
where the time goes:
time: 838 us; the launch traced here: 830 us
  waiting for transfers between devices  402 us (48%)
  matrix products  143 us (17%)
  blocking collectives  96.6 us (12%)
  other arithmetic  66.3 us (8%)
  local copies, waits for them, and re-layouts  49.7 us (6%)
  loops' own time  28.2 us (3%)
  starting transfers between devices  27.7 us (3%)
  between operations  16.3 us (2%)
    psum x1, waiting for transfers between devices, shards(): lax.psum((grad_w_query, grad_w_key, grad_w_value, grad_w_inner, grad_w_ou...  231 us
    psum x1, waiting for transfers between devices, shards(): lax.psum(branch_part.astype(jnp.bfloat16), 'tp').astype(jnp.float32)  56.7 us
    psum x1, waiting for transfers between devices, shards(): lax.psum(product(activ_low, whole_outer).astype(jnp.bfloat16), 'tp')  55.2 us
    psum x1, waiting for transfers between devices, shards(): lax.psum(product_nt(grad_inner_low, whole_inner).astype(jnp.bfloat16), 'tp')  45.5 us
    psum x1, blocking collectives, shards(): lax.psum((grad_w_query, grad_w_key, grad_w_value, grad_w_inner, grad_w_ou...  36 us
    ppermute x5, starting transfers between devices, padded(): lax.ppermute(lax.slice_in_dim(block, block.shape[dim] - width, None, axis...  20.3 us
    dot_general x6, matrix products, product(): return jnp.dot(left, right, preferred_element_type=jnp.float32)  19.3 us
    dot_general x6, matrix products, product_tn(): lax.dot_general(left, right, (((0,), (0,)), ((), ())), preferred_element_...  19.1 us
  transfers between devices with their start and end apart: 17, of which 7 were waited for; matrix products, arithmetic and copies ran while one was open for 7% of the time, Pallas kernels for 0%

commit v1 on v0

v1 whole, which is shorter than its diff:
```python
import math

import jax
import jax.numpy as jnp
from jax import lax
from jax.experimental import pallas as pl
from jax.experimental.pallas import tpu as pltpu
from jax.sharding import PartitionSpec as P

HEAD_DIM = 64
MOST = 512
IDS = 64
NO_ID = 63
LSE_LANE = 60
FAR = -1e30

layer_eps = 1e-12
low = jnp.bfloat16
high = jnp.float32


def nn(left, right):
    return jnp.dot(left, right, preferred_element_type=high)


def nt(left, right):
    return lax.dot_general(left, right, (((1,), (1,)), ((), ())), preferred_element_type=high)


def tn(left, right):
    return lax.dot_general(left, right, (((0,), (0,)), ((), ())), preferred_element_type=high)


def swap(value, axis, bit):
    count = lax.axis_size(axis)
    return lax.ppermute(value, axis, [(i, i ^ bit) for i in range(count)])


def shift(value, axis, step):
    count = lax.axis_size(axis)
    return lax.ppermute(value, axis, [(i, (i + step) % count) for i in range(count)])


def place(whole, part, first):
    return lax.dynamic_update_slice_in_dim(whole, part, first, 0)


def take(whole, first, count):
    return lax.dynamic_slice_in_dim(whole, first, count, 0)


def norm_parts(hidden):
    average = jnp.mean(hidden, axis=-1, keepdims=True)
    centred = hidden - average
    variance = jnp.mean(centred * centred, axis=-1, keepdims=True)
    inverse = lax.rsqrt(variance + layer_eps)
    return centred * inverse, inverse


def norm_back(grad, hat, inverse, gain):
    scaled = grad * gain
    first = jnp.mean(scaled, axis=-1, keepdims=True)
    second = jnp.mean(scaled * hat, axis=-1, keepdims=True)
    return inverse * (scaled - first - hat * second)


def gelu_parts(inner):
    half = 0.5 * (1.0 + lax.erf(inner * 0.7071067811865476))
    slope = half + inner * (jnp.exp(-0.5 * inner * inner) * 0.3989422804014327)
    return inner * half, slope


def three(value):
    first = value.astype(low)
    rest = value - first.astype(high)
    second = rest.astype(low)
    third = (rest - second.astype(high)).astype(low)
    return first, second, third


def meets(seg_q, first_q, size_q, seg_k, first_k, size_k):
    return (seg_q[first_q + size_q - 1] >= seg_k[first_k]) & (
        seg_q[first_q] <= seg_k[first_k + size_k - 1]
    )


def attend_kernel(
    here, seg_q, seg_k, q_ref, k_ref, v_ref, mq_ref, mk_ref, out_ref, full_ref, qa_ref, ka_ref,
    vt_ref, acc_ref, top_ref, *, block, width, heads
):
    parts = out_ref.shape[0]
    keys = k_ref.shape[0]
    scale = 1.0 / math.sqrt(HEAD_DIM)
    mine = here[0]
    for h in range(heads):
        cols = slice(h * HEAD_DIM, (h + 1) * HEAD_DIM)
        ka_ref[h] = jnp.concatenate([k_ref[:, cols], mk_ref[...]], axis=1)
        qa_ref[h] = jnp.concatenate([q_ref[:, cols] * jnp.array(scale, low), mq_ref[...]], axis=1)
        vt_ref[h, :HEAD_DIM, :] = v_ref[:, cols].T
        vt_ref[h, HEAD_DIM:, :] = jnp.ones((vt_ref.shape[1] - HEAD_DIM, keys), low)

    def one_part(r, carry):
        first_q = (mine ^ r) * block
        acc_ref[...] = jnp.zeros_like(acc_ref)
        top_ref[...] = jnp.full_like(top_ref, 2 * FAR)

        def one_block(b, carry):
            first_k = b * width

            @pl.when(meets(seg_q, first_q, block, seg_k, first_k, width))
            def _():
                for h in range(heads):
                    scores = nt(ka_ref[h, pl.ds(first_k, width), :], qa_ref[h, pl.ds(first_q, block), :])
                    top = top_ref[h]
                    peak = jnp.maximum(top, jnp.max(scores, axis=0, keepdims=True))
                    weights = jnp.exp(scores - peak).astype(low)
                    acc_ref[h] = acc_ref[h] * jnp.exp(top - peak) + nn(
                        vt_ref[h, :, pl.ds(first_k, width)], weights
                    )
                    top_ref[h] = peak

            return carry

        lax.fori_loop(0, keys // width, one_block, 0)
        outs = []
        for h in range(heads):
            acc = acc_ref[h]
            total = acc[HEAD_DIM : HEAD_DIM + 1]
            lse = top_ref[h] + jnp.log(total)
            rows = jnp.concatenate(
                [acc[:HEAD_DIM] / total, jnp.broadcast_to(lse, (HEAD_DIM, block))], axis=0
            )
            turned = rows.T
            outs.append(turned[:, :HEAD_DIM])
            minus = three(-turned[:, HEAD_DIM:])
            lane = lax.broadcasted_iota(jnp.int32, (block, HEAD_DIM), 1)
            mask = mq_ref[pl.ds(first_q, block), :].astype(high)
            for i in range(3):
                mask = jnp.where(lane == LSE_LANE + i, minus[i].astype(high), mask)
            qa_ref[h, pl.ds(first_q, block), HEAD_DIM:] = mask.astype(low)
        joined = jnp.concatenate(outs, axis=1)
        full_ref[pl.ds(first_q, block), :] = joined
        out_ref[r] = joined.astype(low)
        return carry

    lax.fori_loop(0, parts, one_part, 0)


def attend(here, seg_q, seg_k, queries, keys, values, mask_q, mask_k, parts):
    rows, local = queries.shape
    count = keys.shape[0]
    heads = local // HEAD_DIM
    block = rows // parts
    width = 256
    vmem = pl.BlockSpec(memory_space=pltpu.VMEM)
    smem = pl.BlockSpec(memory_space=pltpu.SMEM)
    pairs = rows * 768 * heads
    return pl.pallas_call(
        lambda *refs: attend_kernel(*refs, block=block, width=width, heads=heads),
        name="attend",
        out_shape=(
            jax.ShapeDtypeStruct((parts, block, local), low),
            jax.ShapeDtypeStruct((rows, local), high),
            jax.ShapeDtypeStruct((heads, rows, 2 * HEAD_DIM), low),
            jax.ShapeDtypeStruct((heads, count, 2 * HEAD_DIM), low),
        ),
        in_specs=[smem] * 3 + [vmem] * 5,
        out_specs=(vmem,) * 4,
        scratch_shapes=[
            pltpu.VMEM((heads, HEAD_DIM + 16, count), low),
            pltpu.VMEM((heads, HEAD_DIM + 16, block), high),
            pltpu.VMEM((heads, 1, block), high),
        ],
        cost_estimate=pl.CostEstimate(flops=pairs * 256, transcendentals=pairs, bytes_accessed=8 << 20),
    )(here, seg_q, seg_k, queries, keys, values, mask_q, mask_k)


def attend_back_kernel(
    here, seg_q, seg_k, g_ref, full_ref, qa_ref, ka_ref, v_ref, dq_ref, dk_ref, dv_ref, kt_ref,
    va_ref, ga_ref, dka_ref, dva_ref, dqa_ref, *, block, width, heads
):
    parts = g_ref.shape[0]
    keys = v_ref.shape[0]
    scale = 1.0 / math.sqrt(HEAD_DIM)
    mine = here[0]
    for h in range(heads):
        cols = slice(h * HEAD_DIM, (h + 1) * HEAD_DIM)
        kt_ref[h] = ka_ref[h, :, :HEAD_DIM].T
        va_ref[h] = jnp.concatenate([v_ref[:, cols], jnp.ones((keys, HEAD_DIM), low)], axis=1)
    dka_ref[...] = jnp.zeros_like(dka_ref)
    dva_ref[...] = jnp.zeros_like(dva_ref)

    def one_part(r, carry):
        first_q = (mine ^ r) * block
        for h in range(heads):
            cols = slice(h * HEAD_DIM, (h + 1) * HEAD_DIM)
            grad = g_ref[r, :, cols]
            delta = jnp.sum(
                grad.astype(high) * full_ref[pl.ds(first_q, block), cols], axis=1, keepdims=True
            )
            lane = lax.broadcasted_iota(jnp.int32, (block, HEAD_DIM), 1)
            extra = jnp.zeros((block, HEAD_DIM), high)
            for i, piece in enumerate(three(-delta)):
                extra = jnp.where(lane == i, piece.astype(high), extra)
            ga_ref[h] = jnp.concatenate([grad, extra.astype(low)], axis=1)
        dqa_ref[...] = jnp.zeros_like(dqa_ref)

        def one_block(b, carry):
            first_k = b * width

            @pl.when(meets(seg_q, first_q, block, seg_k, first_k, width))
            def _():
                for h in range(heads):
                    span = pl.ds(first_k, width)
                    asks = qa_ref[h, pl.ds(first_q, block), :]
                    probs = jnp.exp(nt(ka_ref[h, span, :], asks))
                    slopes = (probs * nt(va_ref[h, span, :], ga_ref[h])).astype(low)
                    dva_ref[h, span, :] += nn(probs.astype(low), ga_ref[h, :, :HEAD_DIM])
                    dka_ref[h, span, :] += nn(slopes, asks[:, :HEAD_DIM])
                    dqa_ref[h] += nn(kt_ref[h, :, span], slopes)

            return carry

        lax.fori_loop(0, keys // width, one_block, 0)
        dq_ref[pl.ds(first_q, block), :] = jnp.concatenate(
            [(dqa_ref[h] * scale).T for h in range(heads)], axis=1
        ).astype(low)
        return carry

    lax.fori_loop(0, parts, one_part, 0)
    for h in range(heads):
        cols = slice(h * HEAD_DIM, (h + 1) * HEAD_DIM)
        dk_ref[:, cols] = dka_ref[h].astype(low)
        dv_ref[:, cols] = dva_ref[h].astype(low)


def attend_back(here, seg_q, seg_k, grads, full, asks, keys, values):
    parts, block, local = grads.shape
    rows = parts * block
    count = values.shape[0]
    heads = local // HEAD_DIM
    width = 256
    vmem = pl.BlockSpec(memory_space=pltpu.VMEM)
    smem = pl.BlockSpec(memory_space=pltpu.SMEM)
    pairs = rows * 768 * heads
    return pl.pallas_call(
        lambda *refs: attend_back_kernel(*refs, block=block, width=width, heads=heads),
        name="attend_back",
        out_shape=(
            jax.ShapeDtypeStruct((rows, local), low),
            jax.ShapeDtypeStruct((count, local), low),
            jax.ShapeDtypeStruct((count, local), low),
        ),
        in_specs=[smem] * 3 + [vmem] * 5,
        out_specs=(vmem,) * 3,
        scratch_shapes=[
            pltpu.VMEM((heads, HEAD_DIM, count), low),
            pltpu.VMEM((heads, count, 2 * HEAD_DIM), low),
            pltpu.VMEM((heads, block, 2 * HEAD_DIM), low),
            pltpu.VMEM((heads, count, HEAD_DIM), high),
            pltpu.VMEM((heads, count, HEAD_DIM), high),
            pltpu.VMEM((heads, HEAD_DIM, block), high),
        ],
        cost_estimate=pl.CostEstimate(flops=pairs * 640, transcendentals=pairs, bytes_accessed=8 << 20),
    )(here, seg_q, seg_k, grads, full, asks, keys, values)


def gather_fast(shard, f, c):
    rows = shard.shape[0]
    half = rows // 2
    n_f = lax.axis_size("fsdp")
    own = take(shard, c * half, half)
    whole = jnp.zeros((n_f * rows,) + shard.shape[1:], shard.dtype)
    whole = place(whole, shard, f * rows)
    for s in range(1, n_f):
        got = shift(own, "fsdp", s)
        other = swap(got, "ctx", 1)
        first = (f - s) % n_f * rows
        whole = place(whole, got, first + c * half)
        whole = place(whole, other, first + (1 - c) * half)
    return whole


def halo_of(value, c, span):
    rows = value.shape[0]
    return take(value, (1 - c) * (rows - span), span)


def shards(
    inputs, segments, w_query, b_query, w_key, w_value, b_value, w_out, b_out, gain_one, shift_one,
    w_inner, b_inner, w_outer, b_outer, gain_two, shift_two, grad_output,
):
    rows, width = inputs.shape
    local = w_query.shape[1]
    hidden = w_inner.shape[1]
    n_f, n_c, n_t = (lax.axis_size(a) for a in ("fsdp", "ctx", "tp"))
    f, c, t = (lax.axis_index(a) for a in ("fsdp", "ctx", "tp"))
    tokens = rows // n_t
    rim = MOST
    quick = n_f == 4 and n_c == 2 and n_t == 4
    piece = width // n_f
    flip = [t ^ r for r in range(n_t)]

    bundle_a = jnp.concatenate([w_query, w_key, w_value, w_out.T], axis=1)
    if quick:
        whole_a = gather_fast(bundle_a, f, c)
    else:
        whole_a = lax.all_gather(bundle_a, "fsdp", axis=0, tiled=True)
    bundle_f = jnp.concatenate([w_inner, w_outer.T], axis=1)
    bias_row = jnp.pad(b_inner[None], ((0, 7), (0, hidden)))
    if quick:
        half = piece // 2
        own = take(bundle_f, c * half, half)
        base = jnp.zeros((width + 8, 2 * hidden), low)
        near = place(place(base, bias_row, width), bundle_f, f * piece)
        far_own = swap(jnp.concatenate([bundle_f, bias_row], axis=0), "tp", 2)
        far = place(place(base, far_own[piece:], width), far_own[:piece], f * piece)
        for s in range(1, n_f):
            first = (f - s) % n_f * piece
            got = shift(own, "fsdp", s)
            side = swap(got, "ctx", 1)
            got_x = swap(got, "tp", 2)
            side_x = swap(side, "tp", 2) if s == 2 else swap(got_x, "ctx", 1)
            near = place(place(near, got, first + c * half), side, first + (1 - c) * half)
            far = place(place(far, got_x, first + c * half), side_x, first + (1 - c) * half)
        pieces_f = [near, swap(near, "tp", 1), far, swap(far, "tp", 1)]
    else:
        gathered = lax.all_gather(bundle_f, "fsdp", axis=0, tiled=True)
        gathered = lax.all_gather(jnp.concatenate([gathered, bias_row], axis=0), "tp", axis=0)
        pieces_f = [lax.dynamic_index_in_dim(gathered, i, 0, keepdims=False) for i in flip]
    w_in = [p[:width, :hidden] for p in pieces_f]
    w_ot = [p[:width, hidden:] for p in pieces_f]
    b_in = [p[width : width + 1, :hidden].astype(high) for p in pieces_f]

    seg_own = segments.reshape(rows)
    if n_c == 2:
        sent = halo_of(inputs, c, rim)
        if quick:
            part = rim // 2
            got = swap(take(sent, (t & 1) * part, part), "ctx", 1)
            mate = swap(got, "tp", 1)
            even = (t & 1) == 0
            halo_in = jnp.concatenate([jnp.where(even, got, mate), jnp.where(even, mate, got)], axis=0)
        else:
            halo_in = swap(sent, "ctx", 1)
        halo_seg = swap(halo_of(seg_own, c, rim), "ctx", 1)
    else:
        ahead = [(i, i + 1) for i in range(n_c - 1)]
        behind = [(i + 1, i) for i in range(n_c - 1)]

        def both(value):
            return jnp.concatenate(
                [
                    lax.ppermute(value[rows - rim :], "ctx", ahead),
                    lax.ppermute(value[:rim], "ctx", behind),
                ],
                axis=0,
            )

        halo_in = both(inputs)
        halo_seg = both(seg_own + 1) - 1
        halo_seg = jnp.where(halo_seg < 0, NO_ID, halo_seg)
    w_qkv = whole_a[:, : 3 * local]
    bias = jnp.concatenate([b_query, jnp.zeros_like(b_query), b_value]).astype(high)
    own_qkv = (nn(inputs, w_qkv) + bias).astype(low)
    halo_kv = (nn(halo_in, w_qkv[:, local:]) + bias[local:]).astype(low)
    queries = own_qkv[:, :local]
    keys = jnp.concatenate([own_qkv[:, local : 2 * local], halo_kv[:, :local]], axis=0)
    values = jnp.concatenate([own_qkv[:, 2 * local :], halo_kv[:, local:]], axis=0)
    seg_all = jnp.concatenate([seg_own, halo_seg])
    lane = jnp.arange(IDS)
    near_id = seg_all[:, None] == lane
    mask_k = (near_id | ((lane >= LSE_LANE) & (lane < LSE_LANE + 3))).astype(low)
    mask_q = jnp.where(near_id[:rows] | ((lane >= LSE_LANE) & (lane < LSE_LANE + 3)), 0.0, FAR).astype(low)
    here = t.reshape(1)
    attended, full, asks, keys_wide = attend(
        here, seg_own, seg_all, queries, keys, values, mask_q, mask_k, n_t
    )

    w_o = whole_a[:, 3 * local :]
    w_o_near = [w_o] + [swap(w_o, "tp", r) for r in range(1, n_t)]
    w_o_all = jnp.concatenate(w_o_near, axis=1)
    att = jnp.concatenate([attended[0]] + [swap(attended[r], "tp", r) for r in range(1, n_t)], axis=1)
    gain_one_f, shift_one_f, gain_two_f, shift_two_f = (
        v.astype(high) for v in (gain_one, shift_one, gain_two, shift_two)
    )
    first_row = t * tokens
    branch = nt(att, w_o_all) + b_out.astype(high)
    hat_one, inverse_one = norm_parts(take(inputs, first_row, tokens).astype(high) + branch)
    normed = hat_one * gain_one_f + shift_one_f
    normed_low = normed.astype(low)
    acts, slopes = [], []
    outer = b_outer.astype(high)
    for r in range(n_t):
        act, slope = gelu_parts(nn(normed_low, w_in[r]) + b_in[r])
        acts.append(act.astype(low))
        slopes.append(slope)
        outer = outer + nt(acts[r], w_ot[r])
    hat_two, inverse_two = norm_parts(normed + outer)
    output = (hat_two * gain_two_f + shift_two_f).astype(low)
    grad = take(grad_output, first_row, tokens).astype(high)
    g_gain_two = jnp.sum(grad * hat_two, axis=0)
    g_shift_two = jnp.sum(grad, axis=0)
    g_two = norm_back(grad, hat_two, inverse_two, gain_two_f)
    g_outer = g_two.astype(low)
    g_b_outer = jnp.sum(g_outer.astype(high), axis=0)
    g_normed = g_two
    g_inner = []
    for r in range(n_t):
        g_inner.append((nn(g_outer, w_ot[r]) * slopes[r]).astype(low))
        g_normed = g_normed + nt(g_inner[r], w_in[r])
    g_gain_one = jnp.sum(g_normed * hat_one, axis=0)
    g_shift_one = jnp.sum(g_normed, axis=0)
    g_one = norm_back(g_normed, hat_one, inverse_one, gain_one_f)
    g_branch = g_one.astype(low)
    g_b_out = jnp.sum(g_branch.astype(high), axis=0)
    g_att = nn(g_branch, w_o_all).astype(low)
    g_b_inner = [jnp.sum(g.astype(high), axis=0) for g in g_inner]

    g_att_heads = jnp.stack(
        [g_att[:, :local]]
        + [swap(g_att[:, r * local : (r + 1) * local], "tp", r) for r in range(1, n_t)]
    )

    def blocks(r):
        return jnp.concatenate([g_inner[r], acts[r], att[:, r * local : (r + 1) * local]], axis=1)

    def weight_grads(norm, g_out, g_br, wide):
        return jnp.concatenate(
            [
                tn(norm, wide[:, :hidden]),
                tn(g_out, wide[:, hidden : 2 * hidden]),
                tn(g_br, wide[:, 2 * hidden :]),
            ],
            axis=1,
        )

    rows_own = jnp.concatenate([normed_low, g_outer, g_branch], axis=1)
    if quick:
        rows_mate = swap(rows_own, "tp", 1)
        grads_f = []
        for r in (0, 2):
            mate = swap(blocks(r + 1), "tp", 1)
            mine = blocks(r)
            parts = []
            for i in range(3):
                cols = slice(i * width, (i + 1) * width)
                units = slice(min(i * hidden, 2 * hidden), (i + 1) * hidden if i < 2 else 2 * hidden + local)
                parts.append(
                    tn(rows_own[:, cols], mine[:, units]) + tn(rows_mate[:, cols], mate[:, units])
                )
            grads_f.append(jnp.concatenate(parts, axis=1).astype(low))
        near_g, far_g = grads_f
        wide = near_g.shape[1]
        mid = width // 2
        quarters = mid // piece
        part_a = near_g[:mid] + swap(far_g[:mid], "tp", 2)
        both_b = jnp.stack([near_g[mid:], far_g[mid:]]).reshape(2, quarters, 2, half, wide)
        keep_b = lax.dynamic_index_in_dim(both_b, c, 2, keepdims=False)
        send_b = lax.dynamic_index_in_dim(both_b, 1 - c, 2, keepdims=False)
        both_b = keep_b + swap(send_b, "ctx", 1)
        part_a = part_a.reshape(quarters, 2, half, wide)
        keep_a = lax.dynamic_index_in_dim(part_a, c, 1, keepdims=False)
        send_a = lax.dynamic_index_in_dim(part_a, 1 - c, 1, keepdims=False)
        part_a = keep_a + swap(send_a, "ctx", 1)
        part_b = both_b[0] + swap(both_b[1], "tp", 2)
        all_z = jnp.concatenate([part_a, part_b], axis=0)
        total = lax.dynamic_index_in_dim(all_z, f, 0, keepdims=False).astype(high)
        for s in range(1, n_f):
            total = total + shift(
                lax.dynamic_index_in_dim(all_z, (f + s) % n_f, 0, keepdims=False), "fsdp", s
            ).astype(high)
        total = total.astype(low)
        other = swap(total, "ctx", 1)
        even = c == 0
        shard_f = jnp.concatenate(
            [jnp.where(even, total, other), jnp.where(even, other, total)], axis=0
        ).astype(high)
    else:
        stacked = jnp.stack(
            [weight_grads(normed_low, g_outer, g_branch, blocks(r)) for r in range(n_t)]
        )
        ordered = jnp.stack([lax.dynamic_index_in_dim(stacked, i, 0, keepdims=False) for i in flip])
        mine = lax.psum_scatter(ordered, "tp", scatter_dimension=0, tiled=False)
        mine = lax.psum(mine, ("fsdp", "ctx"))
        shard_f = take(mine, f * piece, piece)

    g_q, g_k, g_v = attend_back(here, seg_own, seg_all, g_att_heads, full, asks, keys_wide, values)
    edge_kv = jnp.concatenate([g_k[rows:], g_v[rows:]], axis=1)
    g_kv = jnp.concatenate([g_k[:rows], g_v[:rows]], axis=1).astype(high)

    def add_edge(first, got):
        return place(g_kv, take(g_kv, first, rim) + got.astype(high), first)

    if n_c == 2:
        g_kv = add_edge((1 - c) * (rows - rim), swap(edge_kv, "ctx", 1))
    else:
        g_kv = add_edge(0, lax.ppermute(edge_kv[rim:], "ctx", ahead))
        g_kv = add_edge(rows - rim, lax.ppermute(edge_kv[:rim], "ctx", behind))
    g_qkv = jnp.concatenate([g_q, g_kv.astype(low)], axis=1)
    g_b_qkv = jnp.sum(g_qkv.astype(high), axis=0)
    g_in_part = nt(g_qkv, w_qkv).astype(low)
    grad_a = tn(inputs, g_qkv)

    if quick:
        pairs = g_in_part.reshape(n_t, tokens, width)
        first_sum = [
            lax.dynamic_index_in_dim(pairs, flip[r], 0, keepdims=False)
            + swap(lax.dynamic_index_in_dim(pairs, flip[r ^ 1], 0, keepdims=False), "tp", 1)
            for r in (0, 2)
        ]
        mine_in = first_sum[0].astype(high) + swap(first_sum[1], "tp", 2).astype(high) + g_one
        mine_in = mine_in.astype(low)
        small_a = grad_a.astype(low).reshape(n_f, 2, half, 3 * local)
        keep = lax.dynamic_index_in_dim(small_a, c, 1, keepdims=False)
        keep = keep + swap(lax.dynamic_index_in_dim(small_a, 1 - c, 1, keepdims=False), "ctx", 1)
        total = lax.dynamic_index_in_dim(keep, f, 0, keepdims=False).astype(high)
        for s in range(1, n_f):
            total = total + shift(
                lax.dynamic_index_in_dim(keep, (f + s) % n_f, 0, keepdims=False), "fsdp", s
            ).astype(high)
        total = total.astype(low)
        other = swap(total, "ctx", 1)
        shard_a = jnp.concatenate(
            [jnp.where(even, total, other), jnp.where(even, other, total)], axis=0
        ).astype(high)

        def everyone(value):
            far_value = swap(value, "tp", 2)
            duo = jnp.stack([value, far_value])
            mates = swap(duo, "tp", 1)
            result = jnp.zeros((n_t,) + value.shape, value.dtype)
            for r, v in enumerate((duo[0], mates[0], duo[1], mates[1])):
                result = lax.dynamic_update_index_in_dim(result, v, flip[r], 0)
            return result.reshape((n_t * value.shape[0],) + value.shape[1:])

        output = everyone(output)
        grad_inputs = everyone(mine_in).astype(high)
    else:
        mine_in = lax.psum_scatter(
            g_in_part.astype(high).reshape(n_t, tokens, width), "tp", scatter_dimension=0, tiled=False
        )
        grad_inputs = lax.all_gather((mine_in + g_one).astype(low), "tp", axis=0, tiled=True).astype(high)
        output = lax.all_gather(output, "tp", axis=0, tiled=True)
        shard_a = take(lax.psum(grad_a, ("fsdp", "ctx")), f * piece, piece)

    shared = jnp.stack([g_b_out, g_gain_one, g_shift_one, g_b_outer, g_gain_two, g_shift_two])
    stacked = jnp.stack(g_b_inner)
    if quick:
        pair = jnp.concatenate([shared, stacked[0:1], stacked[2:3]], axis=0)
        away = jnp.concatenate([shared, stacked[1:2], stacked[3:4]], axis=0)
        pair = pair + swap(away, "tp", 1)
        away = jnp.concatenate([pair[:6], pair[7:8]], axis=0)
        pair = pair[:7] + swap(away, "tp", 2)
        qv = jnp.pad(g_b_qkv[None], ((0, 0), (0, width - 3 * local)))
        pair = jnp.concatenate([pair, qv], axis=0)
        pair = pair + swap(pair, "ctx", 1)
        pair = pair + swap(pair, "fsdp", 1)
        pair = pair + swap(pair, "fsdp", 2)
        shared, s_b_inner, s_qkv = pair[:6], pair[6], pair[7, : 3 * local]
    else:
        ordered = jnp.stack([lax.dynamic_index_in_dim(stacked, i, 0, keepdims=False) for i in flip])
        s_b_inner = lax.psum(lax.psum_scatter(ordered, "tp", scatter_dimension=0, tiled=False), ("fsdp", "ctx"))
        shared = lax.psum(shared, ("fsdp", "ctx", "tp"))
        s_qkv = lax.psum(g_b_qkv, ("fsdp", "ctx"))
    return (
        output,
        grad_inputs,
        shard_a[:, :local],
        s_qkv[:local],
        shard_a[:, local : 2 * local],
        shard_a[:, 2 * local :],
        s_qkv[2 * local :],
        shard_f[:, 2 * hidden :].T,
        shared[0],
        shared[1],
        shared[2],
        shard_f[:, :hidden],
        s_b_inner,
        shard_f[:, hidden : 2 * hidden].T,
        shared[3],
        shared[4],
        shared[5],
    )


def solution(mesh):
    rows = P(("fsdp", "ctx"), None)
    down, flat, across = P("fsdp", "tp"), P("tp"), P("tp", "fsdp")
    return jax.shard_map(
        shards,
        mesh=mesh,
        in_specs=(
            rows, P("fsdp", "ctx"), down, flat, down, down, flat, across, P(), P(), P(), down, flat,
            across, P(), P(), P(), rows,
        ),
        out_specs=(
            rows, rows, down, flat, down, down, flat, across, P(), P(), P(), down, flat, across,
            P(), P(), P(),
        ),
        check_vma=False,
    )
```

time: 838 us -> 455 us (0.54)
  waiting for transfers between devices: 402 us -> 151 us
  blocking collectives: 96.6 us -> 0 us
  matrix products: 143 us -> 51.7 us
  Pallas kernels: 0 us -> 48.4 us
  local copies, waits for them, and re-layouts: 49.7 us -> 95 us
  starting transfers between devices: 27.7 us -> 57.4 us
  loops' own time: 28.2 us -> 0 us
  other arithmetic: 66.3 us -> 44.5 us
  between operations: 16.3 us -> 2.29 us
    psum x5 -> x0, waiting for transfers between devices: 399 us -> none  [the longest x1 231 us: shards(): lax.psum((grad_w_query, grad_w_key, grad_w_value, grad_w_inner, grad_w_ou...]
    ppermute x10 -> x62, waiting for transfers between devices: 2.15 us -> 151 us  [the longest x50 106 us: swap(): return lax.ppermute(value, axis, [(i, i ^ bit) for i in range(count)])]
    dot_general x46 -> x34, matrix products: 143 us -> 51.7 us  [the longest x13 24 us: tn(): lax.dot_general(left, right, (((0,), (0,)), ((), ())), preferred_element_...]
    all_gather x4 -> x0, blocking collectives: 60.7 us -> none  [the longest x1 15.5 us: shards(): lax.all_gather(w_value, 'fsdp', axis=0, tiled=True)]
    pallas_call x0 -> x2, Pallas kernels: none -> 48.4 us  [the longest x1 24.4 us: attend(): pl.pallas_call(lambda *refs: attend_kernel(*refs, block=block, width=widt...]
    dynamic_update_slice x0 -> x28, local copies, waits for them, and re-layouts: none -> 42.7 us  [the longest x22 34.4 us: place(): return lax.dynamic_update_slice_in_dim(whole, part, first, 0)]
    psum x1 -> x0, blocking collectives: 36 us -> none  [shards(): lax.psum((grad_w_query, grad_w_key, grad_w_value, grad_w_inner, grad_w_ou...]
    reduce_sum x16 -> x6, other arithmetic: 37.7 us -> 5.7 us  [the longest x1 2.05 us: shards(): g_b_out = jnp.sum(g_branch.astype(high), axis=0)]
  transfers between devices with their start and end apart: 17 -> 62, of which waited for: 7 -> 27; matrix products, arithmetic and copies ran while one was open for 7% -> 33% of each run, Pallas kernels for 0% -> 11%
where the time goes in v1:
time: 455 us; the launch traced here: 450 us
  waiting for transfers between devices  151 us (33%)
  local copies, waits for them, and re-layouts  95 us (21%)
  starting transfers between devices  57.4 us (13%)
  matrix products  51.7 us (11%)
  Pallas kernels  48.4 us (11%)
  other arithmetic  44.5 us (10%)
    ppermute x50, waiting for transfers between devices, swap(): return lax.ppermute(value, axis, [(i, i ^ bit) for i in range(count)])  106 us
    ppermute x12, waiting for transfers between devices, shift(): lax.ppermute(value, axis, [(i, (i + step) % count) for i in range(count)])  44.5 us
    ppermute x50, starting transfers between devices, swap(): return lax.ppermute(value, axis, [(i, i ^ bit) for i in range(count)])  44 us
    dynamic_update_slice x22, local copies, waits for them, and re-layouts, place(): return lax.dynamic_update_slice_in_dim(whole, part, first, 0)  34.4 us
    pallas_call x1, Pallas kernels, attend(): pl.pallas_call(lambda *refs: attend_kernel(*refs, block=block, width=widt...  24.4 us
    dot_general x13, matrix products, tn(): lax.dot_general(left, right, (((0,), (0,)), ((), ())), preferred_element_...  24 us
    pallas_call x1, Pallas kernels, attend_back(): pl.pallas_call(lambda *refs: attend_back_kernel(*refs, block=block, width...  24 us
    dot_general x11, matrix products, nn(): return jnp.dot(left, right, preferred_element_type=high)  15.1 us
  transfers between devices with their start and end apart: 62, of which 27 were waited for; matrix products, arithmetic and copies ran while one was open for 33% of the time, Pallas kernels for 11%

profile of v1, /device:TPU:10, one launch (start us, length us, event | category | flops | bytes accessed | tf_op | source)
XLA Modules:
  0.0 449.9 jit_solution(12341514854066850579)
XLA Ops:
  8.3 1.8 collective-permute-start.5
  13.9 1.9 constant_dynamic-slice_fusion
  17.8 5.0 %dynamic_update_slice.97 = bf16[768,768]{0,1:T(8,128)(2,1)} dynamic-update-slice(bf16[768,768]{0,1:T(8,128)(2,1)} %broadcast_in_dim.28, bf16[192,768]{0,1:T(8,128)(2,1)S(1)} %pad_maximum_fusion.16, s32[]{:T(128)S(6)} %select_n.204, s32[]{:T(128)} %constant.172.clone.1) | dynamic-update-slice | bytes 589828 | tf_op jit(solution)/shard_map/dynamic_update_slice | solution.py:45
  22.8 2.9 collective-permute-start.17
  28.9 9.8 %collective-permute-done.5 = bf16[96,768]{0,1:T(8,128)(2,1)} collective-permute-done((bf16[96,768]{0,1:T(8,128)(2,1)}, bf16[96,768]{0,1:T(8,128)(2,1)}, u32[]{:S(2)}, u32[]{:S(2)}) %collective-permute-start.5) | collective-permute-done | bytes 147488 | tf_op jit(solution)/shard_map/ppermute | solution.py:41
  41.1 3.4 dynamic_update_slice.98
  45.1 3.7 dynamic_update_slice.99
  48.8 3.9 dynamic_update_slice.100
  52.8 3.1 dynamic_update_slice.101
  55.9 3.4 dynamic_update_slice.102
  59.9 3.8 dynamic_update_slice.103
  63.7 4.0 fusion
  67.7 2.7 collective-permute-start.16
  73.5 3.3 collective-permute-done.16
  81.2 3.3 collective-permute-done.18
  87.0 4.5 collective-permute-done.20
  93.8 7.8 %collective-permute-done.23 = bf16[96,1536]{1,0:T(8,128)(2,1)} collective-permute-done((bf16[96,1536]{1,0:T(8,128)(2,1)}, bf16[96,1536]{1,0:T(8,128)(2,1)}, u32[]{:S(2)}, u32[]{:S(2)}) %collective-permute-start.23) | collective-permute-done | bytes 294944 | tf_op jit(solution)/shard_map/ppermute | solution.py:36
  109.2 24.4 %attend.1 = (bf16[4,384,192]{2,1,0:T(8,128)(2,1)}, f32[1536,192]{1,0:T(8,128)}, bf16[3,1536,128]{2,1,0:T(8,128)(2,1)}, bf16[3,2048,128]{2,1,0:T(8,128)(2,1)}) custom-call(s32[1]{0:T(128)} %bitcast.refs_0_, s32[1536]{0:T(1024)} %copy-done.38, s32[2048]{0:T(1024)} %copy-done.37, bf16[1536,192]{1,0:T(8,128)(2,1)} %get-tuple-element.131.refs_3_, ...), custom_call_target="tpu_custom_call" | custom-call | flops 905969664 | bytes 8388608 | tf_op jit(solution)/shard_map/attend/pallas_call | solution.py:158
  138.6 5.4 %collective-permute-done.26 = bf16[96,1536]{1,0:T(8,128)(2,1)S(1)} collective-permute-done((bf16[96,1536]{1,0:T(8,128)(2,1)S(1)}, bf16[96,1536]{1,0:T(8,128)(2,1)S(1)}, u32[]{:S(2)}, u32[]{:S(2)}) %collective-permute-start.26) | collective-permute-done | bytes 294944 | tf_op jit(solution)/shard_map/ppermute | solution.py:36
  147.3 3.4 collective-permute-done.28
  154.6 2.2 fusion.126
  168.8 2.3 fusion.118
  171.9 2.2 fusion.130
  175.6 2.5 fusion.128
  185.7 2.1 convert_reduce_fusion.7
  189.3 2.2 fusion.116
  192.6 2.5 copy.77
  207.9 2.1 convolution_convert_fusion.2
  217.2 2.6 copy.76
  223.7 2.2 pad_maximum_fusion.11.refs_3_
  225.9 24.0 %attend_back.1 = (bf16[1536,192]{1,0:T(8,128)(2,1)}, bf16[2048,192]{1,0:T(8,128)(2,1)}, bf16[2048,192]{1,0:T(8,128)(2,1)}) custom-call(s32[1]{0:T(128)} %bitcast.refs_0_, s32[1536]{0:T(1024)} %copy-done.38, s32[2048]{0:T(1024)} %copy-done.37, bf16[4,384,192]{2,1,0:T(8,128)(2,1)} %pad_maximum_fusion.11.refs_3_, f32[1536,192]{1,0:T(8,128)} %get-tuple-element.25.refs_4_, ...), custom_call_target="tpu_custom_call" | custom-call | flops 2264924160 | bytes 8388608 | tf_op jit(solution)/shard_map/attend_back/pallas_call | solution.py:246
  252.1 2.7 collective-permute-start.35
  255.3 8.2 %collective-permute-done.35 = bf16[512,384]{1,0:T(8,128)(2,1)S(1)} collective-permute-done((bf16[512,384]{1,0:T(8,128)(2,1)S(1)}, bf16[512,384]{1,0:T(8,128)(2,1)S(1)}, u32[]{:S(2)}, u32[]{:S(2)}) %collective-permute-start.35) | collective-permute-done | bytes 393248 | tf_op jit(solution)/shard_map/ppermute | solution.py:36
  265.8 2.8 fusion.19
  268.6 3.5 convolution_convert_fusion
  272.1 1.8 collective-permute-start.48
  276.1 2.2 dynamic-slice_bitcast_fusion.2
  279.9 2.0 collective-permute-start.50
  281.9 2.4 pad_maximum_fusion.7
  284.7 2.3 collective-permute-done.41
  289.1 5.4 %collective-permute-done.42 = bf16[96,576]{1,0:T(8,128)(2,1)S(1)} collective-permute-done((bf16[96,576]{1,0:T(8,128)(2,1)S(1)}, bf16[96,576]{1,0:T(8,128)(2,1)S(1)}, u32[]{:S(2)}, u32[]{:S(2)}) %collective-permute-start.42) | collective-permute-done | bytes 110624 | tf_op jit(solution)/shard_map/ppermute | solution.py:41
  295.3 2.0 collective-permute-done.43
  297.3 2.8 collective-permute-done.44
  301.6 1.9 bitcast_add_fusion.1
  303.6 2.5 collective-permute-done.45
  308.2 2.2 add_convert_fusion.2
  310.4 2.1 add_convert_fusion.1
  318.7 1.9 add_convert_fusion.4
  320.5 1.8 add_convert_fusion.3
  326.0 24.7 %collective-permute-done.54 = bf16[384,1728]{0,1:T(8,128)(2,1)} collective-permute-done((bf16[384,1728]{0,1:T(8,128)(2,1)}, bf16[384,1728]{0,1:T(8,128)(2,1)}, u32[]{:S(2)}, u32[]{:S(2)}) %collective-permute-start.54) | collective-permute-done | bytes 1327136 | tf_op jit(solution)/shard_map/ppermute | solution.py:36
  350.7 3.9 fusion.121
  362.4 2.1 slice_dynamic-update-slice_fusion.3
  364.5 1.9 constant_dynamic-update-slice_fusion.2
  366.4 1.9 slice_dynamic-update-slice_fusion.2
  368.3 8.1 %collective-permute-done.39 = bf16[384,768]{1,0:T(8,128)(2,1)S(1)} collective-permute-done((bf16[384,768]{1,0:T(8,128)(2,1)S(1)}, bf16[384,768]{1,0:T(8,128)(2,1)S(1)}, u32[]{:S(2)}, u32[]{:S(2)}) %collective-permute-start.39) | collective-permute-done | bytes 589856 | tf_op jit(solution)/shard_map/ppermute | solution.py:36
  377.7 2.6 copy.78
  382.1 8.9 %collective-permute-done.56 = bf16[2,2,96,1728]{3,2,1,0:T(8,128)(2,1)} collective-permute-done((bf16[2,2,96,1728]{3,2,1,0:T(8,128)(2,1)}, bf16[2,2,96,1728]{3,2,1,0:T(8,128)(2,1)}, u32[]{:S(2)}, u32[]{:S(2)}) %collective-permute-start.56) | collective-permute-done | bytes 1327136 | tf_op jit(solution)/shard_map/ppermute | solution.py:36
  394.4 9.9 %collective-permute-done.55 = bf16[2,96,1728]{2,1,0:T(8,128)(2,1)S(1)} collective-permute-done((bf16[2,96,1728]{2,1,0:T(8,128)(2,1)S(1)}, bf16[2,96,1728]{2,1,0:T(8,128)(2,1)S(1)}, u32[]{:S(2)}, u32[]{:S(2)}) %collective-permute-start.55) | collective-permute-done | bytes 663584 | tf_op jit(solution)/shard_map/ppermute | solution.py:36
  404.4 3.2 collective-permute-done.57
  408.1 2.1 collective-permute-start.58
  412.9 19.6 %collective-permute-done.58 = bf16[96,1728]{1,0:T(8,128)(2,1)S(1)} collective-permute-done((bf16[96,1728]{1,0:T(8,128)(2,1)S(1)}, bf16[96,1728]{1,0:T(8,128)(2,1)S(1)}, u32[]{:S(2)}, u32[]{:S(2)}) %collective-permute-start.58) | collective-permute-done | bytes 331808 | tf_op jit(solution)/shard_map/ppermute | solution.py:41
  432.4 4.0 collective-permute-done.59
  438.5 2.7 bitcast_convert_fusion
  441.2 6.6 %collective-permute-done.61 = bf16[96,1728]{1,0:T(8,128)(2,1)S(1)} collective-permute-done((bf16[96,1728]{1,0:T(8,128)(2,1)S(1)}, bf16[96,1728]{1,0:T(8,128)(2,1)S(1)}, u32[]{:S(2)}, u32[]{:S(2)}) %collective-permute-start.61) | collective-permute-done | bytes 331808 | tf_op jit(solution)/shard_map/ppermute | solution.py:36
  (367 shorter events, 146.8 us)
Async XLA Ops:
  5.5 21.4 %collective-permute-start.1 = (bf16[96,768]{0,1:T(8,128)(2,1)}, bf16[96,768]{0,1:T(8,128)(2,1)}, u32[]{:S(2)}, u32[]{:S(2)}) collective-permute-start(bf16[96,768]{0,1:T(8,128)(2,1)} %constant_dynamic-slice_fusion.1), channel_id=1, source_target_pairs={{0,8},{8,16},{16,24},{24,0},{1,9},{9,17},{17,25},{25,1},{2,10},{10... | collective-permute-start | bytes 442376 | tf_op jit(solution)/shard_map/ppermute | solution.py:41
  7.1 20.3 %collective-permute-start.3 = (bf16[96,768]{0,1:T(8,128)(2,1)}, bf16[96,768]{0,1:T(8,128)(2,1)}, u32[]{:S(2)}, u32[]{:S(2)}) collective-permute-start(bf16[96,768]{0,1:T(8,128)(2,1)} %constant_dynamic-slice_fusion.1), channel_id=1, source_target_pairs={{0,16},{8,24},{16,0},{24,8},{1,17},{9,25},{17,1},{25,9},{2,18},{10... | collective-permute-start | bytes 442376 | tf_op jit(solution)/shard_map/ppermute | solution.py:41
  8.3 30.4 %collective-permute-start.5 = (bf16[96,768]{0,1:T(8,128)(2,1)}, bf16[96,768]{0,1:T(8,128)(2,1)}, u32[]{:S(2)}, u32[]{:S(2)}) collective-permute-start(bf16[96,768]{0,1:T(8,128)(2,1)} %constant_dynamic-slice_fusion.1), channel_id=1, source_target_pairs={{0,24},{8,0},{16,8},{24,16},{1,25},{9,1},{17,9},{25,17},{2,26},{10... | collective-permute-start | bytes 442376 | tf_op jit(solution)/shard_map/ppermute | solution.py:41
  10.2 12.7 %collective-permute-start = (s32[512]{0:T(512)S(1)}, s32[512]{0:T(512)S(1)}, u32[]{:S(2)}, u32[]{:S(2)}) collective-permute-start(s32[512]{0:T(512)S(1)} %bitcast.143), channel_id=1, source_target_pairs={{0,4},{4,0},{1,5},{5,1},{2,6},{6,2},{3,7},{7,3},{8,12},{12,8},{9,1... | collective-permute-start | bytes 6152 | tf_op jit(solution)/shard_map/ppermute | solution.py:36
  12.4 55.3 %collective-permute-start.15 = (bf16[96,1536]{1,0:T(8,128)(2,1)}, bf16[96,1536]{1,0:T(8,128)(2,1)}, u32[]{:S(2)}, u32[]{:S(2)}) collective-permute-start(bf16[96,1536]{1,0:T(8,128)(2,1)} %fusion.101), channel_id=1, source_target_pairs={{0,8},{8,16},{16,24},{24,0},{1,9},{9,17},{17,25},{25,1},{2,10},{10... | collective-permute-start | bytes 884744 | tf_op jit(solution)/shard_map/ppermute | solution.py:41
  22.8 50.6 %collective-permute-start.17 = (bf16[96,1536]{1,0:T(8,128)(2,1)}, bf16[96,1536]{1,0:T(8,128)(2,1)}, u32[]{:S(2)}, u32[]{:S(2)}) collective-permute-start(bf16[96,1536]{1,0:T(8,128)(2,1)} %fusion.101), channel_id=1, source_target_pairs={{0,16},{8,24},{16,0},{24,8},{1,17},{9,25},{17,1},{25,9},{2,18},{10... | collective-permute-start | bytes 884744 | tf_op jit(solution)/shard_map/ppermute | solution.py:41
  25.7 27.0 %copy-start.37 = (s32[2048]{0:T(1024)}, s32[2048]{0:T(1024)S(1)}, u32[]{:S(2)}) copy-start(s32[2048]{0:T(1024)S(1)} %pad_add_fusion.refs_2_) | copy-start | bytes 24580
  26.9 17.7 %collective-permute-start.2 = (bf16[96,768]{0,1:T(8,128)(2,1)}, bf16[96,768]{0,1:T(8,128)(2,1)S(1)}, u32[]{:S(2)}, u32[]{:S(2)}) collective-permute-start(bf16[96,768]{0,1:T(8,128)(2,1)} %collective-permute-done.1), channel_id=1, source_target_pairs={{0,4},{4,0},{1,5},{5,1},{2,6},{6,2},{3,7},{7,3},{8,12},{12,8},{9,1... | collective-permute-start | bytes 442376 | tf_op jit(solution)/shard_map/ppermute | solution.py:36
  27.4 25.3 %collective-permute-start.4 = (bf16[96,768]{0,1:T(8,128)(2,1)}, bf16[96,768]{0,1:T(8,128)(2,1)S(1)}, u32[]{:S(2)}, u32[]{:S(2)}) collective-permute-start(bf16[96,768]{0,1:T(8,128)(2,1)} %collective-permute-done.3), channel_id=1, source_target_pairs={{0,4},{4,0},{1,5},{5,1},{2,6},{6,2},{3,7},{7,3},{8,12},{12,8},{9,1... | collective-permute-start | bytes 442376 | tf_op jit(solution)/shard_map/ppermute | solution.py:36
  38.7 20.6 %collective-permute-start.6 = (bf16[96,768]{0,1:T(8,128)(2,1)}, bf16[96,768]{0,1:T(8,128)(2,1)}, u32[]{:S(2)}, u32[]{:S(2)}) collective-permute-start(bf16[96,768]{0,1:T(8,128)(2,1)} %collective-permute-done.5), channel_id=1, source_target_pairs={{0,4},{4,0},{1,5},{5,1},{2,6},{6,2},{3,7},{7,3},{8,12},{12,8},{9,1... | collective-permute-start | bytes 442376 | tf_op jit(solution)/shard_map/ppermute | solution.py:36
  44.5 35.1 %collective-permute-start.19 = (bf16[96,1536]{1,0:T(8,128)(2,1)}, bf16[96,1536]{1,0:T(8,128)(2,1)}, u32[]{:S(2)}, u32[]{:S(2)}) collective-permute-start(bf16[96,1536]{1,0:T(8,128)(2,1)} %fusion.101), channel_id=1, source_target_pairs={{0,24},{8,0},{16,8},{24,16},{1,25},{9,1},{17,9},{25,17},{2,26},{10... | collective-permute-start | bytes 884744 | tf_op jit(solution)/shard_map/ppermute | solution.py:41
  52.7 40.3 %collective-permute-start.7 = (bf16[256,768]{1,0:T(8,128)(2,1)S(1)}, bf16[256,768]{1,0:T(8,128)(2,1)}, u32[]{:S(2)}, u32[]{:S(2)}) collective-permute-start(bf16[256,768]{1,0:T(8,128)(2,1)S(1)} %copy-done.29), channel_id=1, source_target_pairs={{0,4},{4,0},{1,5},{5,1},{2,6},{6,2},{3,7},{7,3},{8,12},{12,8},{9,1... | collective-permute-start | bytes 1179656 | tf_op jit(solution)/shard_map/ppermute | solution.py:36
  59.3 34.3 %collective-permute-start.22 = (bf16[200,1536]{1,0:T(8,128)(2,1)}, bf16[200,1536]{1,0:T(8,128)(2,1)S(1)}, u32[]{:S(2)}, u32[]{:S(2)}) collective-permute-start(bf16[200,1536]{1,0:T(8,128)(2,1)} %pad_maximum_fusion.13), channel_id=1, source_target_pairs={{0,2},{1,3},{2,0},{3,1},{4,6},{5,7},{6,4},{7,5},{8,10},{9,11},{10,... | collective-permute-start | bytes 1843208 | tf_op jit(solution)/shard_map/ppermute | solution.py:36
  67.7 9.2 %collective-permute-start.16 = (bf16[96,1536]{1,0:T(8,128)(2,1)}, bf16[96,1536]{1,0:T(8,128)(2,1)S(1)}, u32[]{:S(2)}, u32[]{:S(2)}) collective-permute-start(bf16[96,1536]{1,0:T(8,128)(2,1)} %collective-permute-done.15), channel_id=1, source_target_pairs={{0,4},{4,0},{1,5},{5,1},{2,6},{6,2},{3,7},{7,3},{8,12},{12,8},{9,1... | collective-permute-start | bytes 884744 | tf_op jit(solution)/shard_map/ppermute | solution.py:36
  73.5 73.8 %collective-permute-start.12 = (bf16[768,192]{0,1:T(8,128)(2,1)}, bf16[768,192]{0,1:T(8,128)(2,1)}, u32[]{:S(2)}, u32[]{:S(2)}) collective-permute-start(bf16[768,192]{0,1:T(8,128)(2,1)} %slice.322), channel_id=1, source_target_pairs={{0,1},{1,0},{2,3},{3,2},{4,5},{5,4},{6,7},{7,6},{8,9},{9,8},{10,11... | collective-permute-start | bytes 884744 | tf_op jit(solution)/shard_map/ppermute | solution.py:36
  76.9 7.6 %collective-permute-start.18 = (bf16[96,1536]{1,0:T(8,128)(2,1)}, bf16[96,1536]{1,0:T(8,128)(2,1)S(1)}, u32[]{:S(2)}, u32[]{:S(2)}) collective-permute-start(bf16[96,1536]{1,0:T(8,128)(2,1)} %collective-permute-done.17), channel_id=1, source_target_pairs={{0,4},{4,0},{1,5},{5,1},{2,6},{6,2},{3,7},{7,3},{8,12},{12,8},{9,1... | collective-permute-start | bytes 884744 | tf_op jit(solution)/shard_map/ppermute | solution.py:36
  79.6 67.6 %collective-permute-start.13 = (bf16[768,192]{0,1:T(8,128)(2,1)}, bf16[768,192]{0,1:T(8,128)(2,1)}, u32[]{:S(2)}, u32[]{:S(2)}) collective-permute-start(bf16[768,192]{0,1:T(8,128)(2,1)} %slice.322), channel_id=1, source_target_pairs={{0,2},{1,3},{2,0},{3,1},{4,6},{5,7},{6,4},{7,5},{8,10},{9,11},{10,... | collective-permute-start | bytes 884744 | tf_op jit(solution)/shard_map/ppermute | solution.py:36
  84.5 6.9 %collective-permute-start.20 = (bf16[96,1536]{1,0:T(8,128)(2,1)}, bf16[96,1536]{1,0:T(8,128)(2,1)S(1)}, u32[]{:S(2)}, u32[]{:S(2)}) collective-permute-start(bf16[96,1536]{1,0:T(8,128)(2,1)} %collective-permute-done.19), channel_id=1, source_target_pairs={{0,4},{4,0},{1,5},{5,1},{2,6},{6,2},{3,7},{7,3},{8,12},{12,8},{9,1... | collective-permute-start | bytes 884744 | tf_op jit(solution)/shard_map/ppermute | solution.py:36
  91.4 10.2 %collective-permute-start.23 = (bf16[96,1536]{1,0:T(8,128)(2,1)}, bf16[96,1536]{1,0:T(8,128)(2,1)}, u32[]{:S(2)}, u32[]{:S(2)}) collective-permute-start(bf16[96,1536]{1,0:T(8,128)(2,1)} %collective-permute-done.15), channel_id=1, source_target_pairs={{0,2},{1,3},{2,0},{3,1},{4,6},{5,7},{6,4},{7,5},{8,10},{9,11},{10,... | collective-permute-start | bytes 884744 | tf_op jit(solution)/shard_map/ppermute | solution.py:36
  93.0 68.5 %copy-start = (bf16[776,1536]{1,0:T(8,128)(2,1)}, bf16[776,1536]{1,0:T(8,128)(2,1)S(1)}, u32[]{:S(2)}) copy-start(bf16[776,1536]{1,0:T(8,128)(2,1)S(1)} %constant_dynamic-update-slice_fusion.10) | copy-start | bytes 7151620
  93.0 43.3 %collective-permute-start.25 = (bf16[96,1536]{1,0:T(8,128)(2,1)}, bf16[96,1536]{1,0:T(8,128)(2,1)S(1)}, u32[]{:S(2)}, u32[]{:S(2)}) collective-permute-start(bf16[96,1536]{1,0:T(8,128)(2,1)} %collective-permute-done.17), channel_id=1, source_target_pairs={{0,2},{1,3},{2,0},{3,1},{4,6},{5,7},{6,4},{7,5},{8,10},{9,11},{10,... | collective-permute-start | bytes 884744 | tf_op jit(solution)/shard_map/ppermute | solution.py:36
  93.6 10.5 %collective-permute-start.8 = (bf16[256,768]{1,0:T(8,128)(2,1)}, bf16[256,768]{1,0:T(8,128)(2,1)S(1)}, u32[]{:S(2)}, u32[]{:S(2)}) collective-permute-start(bf16[256,768]{1,0:T(8,128)(2,1)} %collective-permute-done.7), channel_id=1, source_target_pairs={{0,1},{1,0},{2,3},{3,2},{4,5},{5,4},{6,7},{7,6},{8,9},{9,8},{10,11... | collective-permute-start | bytes 1179656 | tf_op jit(solution)/shard_map/ppermute | solution.py:36
  101.6 35.4 %collective-permute-start.27 = (bf16[96,1536]{1,0:T(8,128)(2,1)}, bf16[96,1536]{1,0:T(8,128)(2,1)S(1)}, u32[]{:S(2)}, u32[]{:S(2)}) collective-permute-start(bf16[96,1536]{1,0:T(8,128)(2,1)} %collective-permute-done.19), channel_id=1, source_target_pairs={{0,2},{1,3},{2,0},{3,1},{4,6},{5,7},{6,4},{7,5},{8,10},{9,11},{10,... | collective-permute-start | bytes 884744 | tf_op jit(solution)/shard_map/ppermute | solution.py:36
  104.1 30.8 %collective-permute-start.24 = (bf16[96,1536]{1,0:T(8,128)(2,1)}, bf16[96,1536]{1,0:T(8,128)(2,1)S(1)}, u32[]{:S(2)}, u32[]{:S(2)}) collective-permute-start(bf16[96,1536]{1,0:T(8,128)(2,1)} %collective-permute-done.23), channel_id=1, source_target_pairs={{0,4},{4,0},{1,5},{5,1},{2,6},{6,2},{3,7},{7,3},{8,12},{12,8},{9,1... | collective-permute-start | bytes 884744 | tf_op jit(solution)/shard_map/ppermute | solution.py:36
  134.9 9.0 %collective-permute-start.26 = (bf16[96,1536]{1,0:T(8,128)(2,1)S(1)}, bf16[96,1536]{1,0:T(8,128)(2,1)S(1)}, u32[]{:S(2)}, u32[]{:S(2)}) collective-permute-start(bf16[96,1536]{1,0:T(8,128)(2,1)S(1)} %copy-done.31), channel_id=1, source_target_pairs={{0,2},{1,3},{2,0},{3,1},{4,6},{5,7},{6,4},{7,5},{8,10},{9,11},{10,... | collective-permute-start | bytes 884744 | tf_op jit(solution)/shard_map/ppermute | solution.py:36
  136.3 15.9 %collective-permute-start.14 = (bf16[768,192]{0,1:T(8,128)(2,1)}, bf16[768,192]{0,1:T(8,128)(2,1)S(1)}, u32[]{:S(2)}, u32[]{:S(2)}) collective-permute-start(bf16[768,192]{0,1:T(8,128)(2,1)} %slice.322), channel_id=1, source_target_pairs={{0,3},{1,2},{2,1},{3,0},{4,7},{5,6},{6,5},{7,4},{8,11},{9,10},{10,... | collective-permute-start | bytes 884744 | tf_op jit(solution)/shard_map/ppermute | solution.py:36
  137.0 22.9 %collective-permute-start.21 = (bf16[776,1536]{1,0:T(8,128)(2,1)S(1)}, bf16[776,1536]{1,0:T(8,128)(2,1)S(1)}, u32[]{:S(2)}, u32[]{:S(2)}) collective-permute-start(bf16[776,1536]{1,0:T(8,128)(2,1)S(1)} %constant_dynamic-update-slice_fusion.10), channel_id=1, source_target_pairs={{0,1},{1,0},{2,3},{3,2},{4,5},{5,4},{6,7},{7,6},{8,9},{9,8},{10,11... | collective-permute-start | bytes 7151624 | tf_op jit(solution)/shard_map/ppermute | solution.py:36
  144.0 6.7 %collective-permute-start.28 = (bf16[96,1536]{1,0:T(8,128)(2,1)S(1)}, bf16[96,1536]{1,0:T(8,128)(2,1)S(1)}, u32[]{:S(2)}, u32[]{:S(2)}) collective-permute-start(bf16[96,1536]{1,0:T(8,128)(2,1)S(1)} %collective-permute-done.27), channel_id=1, source_target_pairs={{0,4},{4,0},{1,5},{5,1},{2,6},{6,2},{3,7},{7,3},{8,12},{12,8},{9,1... | collective-permute-start | bytes 884744 | tf_op jit(solution)/shard_map/ppermute | solution.py:36
  147.2 7.3 %collective-permute-start.10 = (bf16[384,192]{1,0:T(8,128)(2,1)S(1)}, bf16[384,192]{1,0:T(8,128)(2,1)S(1)}, u32[]{:S(2)}, u32[]{:S(2)}) collective-permute-start(bf16[384,192]{1,0:T(8,128)(2,1)S(1)} %get-tuple-element.137), channel_id=1, source_target_pairs={{0,2},{1,3},{2,0},{3,1},{4,6},{5,7},{6,4},{7,5},{8,10},{9,11},{10,... | collective-permute-start | bytes 442376 | tf_op jit(solution)/shard_map/ppermute | solution.py:36
  147.2 7.4 %collective-permute-start.11 = (bf16[384,192]{1,0:T(8,128)(2,1)S(1)}, bf16[384,192]{1,0:T(8,128)(2,1)S(1)}, u32[]{:S(2)}, u32[]{:S(2)}) collective-permute-start(bf16[384,192]{1,0:T(8,128)(2,1)S(1)} %get-tuple-element.136), channel_id=1, source_target_pairs={{0,3},{1,2},{2,1},{3,0},{4,7},{5,6},{6,5},{7,4},{8,11},{9,10},{10,... | collective-permute-start | bytes 442376 | tf_op jit(solution)/shard_map/ppermute | solution.py:36
  150.7 3.9 collective-permute-start.9
  152.2 9.9 %collective-permute-start.29 = (bf16[776,1536]{1,0:T(8,128)(2,1)}, bf16[776,1536]{1,0:T(8,128)(2,1)S(1)}, u32[]{:S(2)}, u32[]{:S(2)}) collective-permute-start(bf16[776,1536]{1,0:T(8,128)(2,1)} %constant_dynamic-update-slice_fusion.4), channel_id=1, source_target_pairs={{0,1},{1,0},{2,3},{3,2},{4,5},{5,4},{6,7},{7,6},{8,9},{9,8},{10,11... | collective-permute-start | bytes 7151624 | tf_op jit(solution)/shard_map/ppermute | solution.py:36
  195.1 111.0 %collective-permute-start.53 = (bf16[384,1728]{0,1:T(8,128)(2,1)}, bf16[384,1728]{0,1:T(8,128)(2,1)}, u32[]{:S(2)}, u32[]{:S(2)}) collective-permute-start(bf16[384,1728]{0,1:T(8,128)(2,1)} %copy.77), channel_id=1, source_target_pairs={{0,1},{1,0},{2,3},{3,2},{4,5},{5,4},{6,7},{7,6},{8,9},{9,8},{10,11... | collective-permute-start | bytes 3981320 | tf_op jit(solution)/shard_map/ppermute | solution.py:36
  207.9 12.1 %collective-permute-start.46 = (f32[8,768]{1,0:T(8,128)}, f32[8,768]{1,0:T(8,128)}, u32[]{:S(2)}, u32[]{:S(2)}) collective-permute-start(f32[8,768]{1,0:T(8,128)} %concatenate.99), channel_id=1, source_target_pairs={{0,1},{1,0},{2,3},{3,2},{4,5},{5,4},{6,7},{7,6},{8,9},{9,8},{10,11... | collective-permute-start | bytes 73736 | tf_op jit(solution)/shard_map/ppermute | solution.py:36
  211.0 10.6 %collective-permute-start.32 = (bf16[384,192]{1,0:T(8,128)(2,1)}, bf16[384,192]{1,0:T(8,128)(2,1)}, u32[]{:S(2)}, u32[]{:S(2)}) collective-permute-start(bf16[384,192]{1,0:T(8,128)(2,1)} %get-tuple-element.148), channel_id=1, source_target_pairs={{0,1},{1,0},{2,3},{3,2},{4,5},{5,4},{6,7},{7,6},{8,9},{9,8},{10,11... | collective-permute-start | bytes 442376 | tf_op jit(solution)/shard_map/ppermute | solution.py:36
  211.5 10.7 %collective-permute-start.33 = (bf16[384,192]{1,0:T(8,128)(2,1)}, bf16[384,192]{1,0:T(8,128)(2,1)}, u32[]{:S(2)}, u32[]{:S(2)}) collective-permute-start(bf16[384,192]{1,0:T(8,128)(2,1)} %get-tuple-element.147), channel_id=1, source_target_pairs={{0,2},{1,3},{2,0},{3,1},{4,6},{5,7},{6,4},{7,5},{8,10},{9,11},{10,... | collective-permute-start | bytes 442376 | tf_op jit(solution)/shard_map/ppermute | solution.py:36
  212.0 11.7 %collective-permute-start.34 = (bf16[384,192]{1,0:T(8,128)(2,1)}, bf16[384,192]{1,0:T(8,128)(2,1)}, u32[]{:S(2)}, u32[]{:S(2)}) collective-permute-start(bf16[384,192]{1,0:T(8,128)(2,1)} %get-tuple-element.146), channel_id=1, source_target_pairs={{0,3},{1,2},{2,1},{3,0},{4,7},{5,6},{6,5},{7,4},{8,11},{9,10},{10,... | collective-permute-start | bytes 442376 | tf_op jit(solution)/shard_map/ppermute | solution.py:36
  220.0 86.7 %collective-permute-start.51 = (bf16[384,2304]{1,0:T(8,128)(2,1)}, bf16[384,2304]{1,0:T(8,128)(2,1)}, u32[]{:S(2)}, u32[]{:S(2)}) collective-permute-start(bf16[384,2304]{1,0:T(8,128)(2,1)} %pad_maximum_fusion.3), channel_id=1, source_target_pairs={{0,1},{1,0},{2,3},{3,2},{4,5},{5,4},{6,7},{7,6},{8,9},{9,8},{10,11... | collective-permute-start | bytes 5308424 | tf_op jit(solution)/shard_map/ppermute | solution.py:36
  221.6 58.3 %collective-permute-start.30 = (bf16[384,768]{1,0:T(8,128)(2,1)}, bf16[384,768]{1,0:T(8,128)(2,1)}, u32[]{:S(2)}, u32[]{:S(2)}) collective-permute-start(bf16[384,768]{1,0:T(8,128)(2,1)} %get-tuple-element.122), channel_id=1, source_target_pairs={{0,2},{1,3},{2,0},{3,1},{4,6},{5,7},{6,4},{7,5},{8,10},{9,11},{10,... | collective-permute-start | bytes 1769480 | tf_op jit(solution)/shard_map/ppermute | solution.py:36
  222.2 32.6 %collective-permute-start.47 = (f32[7,768]{1,0:T(8,128)S(1)}, f32[7,768]{1,0:T(8,128)S(1)}, u32[]{:S(2)}, u32[]{:S(2)}) collective-permute-start(f32[7,768]{1,0:T(8,128)S(1)} %pad_maximum_fusion.21), channel_id=1, source_target_pairs={{0,2},{1,3},{2,0},{3,1},{4,6},{5,7},{6,4},{7,5},{8,10},{9,11},{10,... | collective-permute-start | bytes 64520 | tf_op jit(solution)/shard_map/ppermute | solution.py:36
  252.1 11.4 %collective-permute-start.35 = (bf16[512,384]{1,0:T(8,128)(2,1)S(1)}, bf16[512,384]{1,0:T(8,128)(2,1)S(1)}, u32[]{:S(2)}, u32[]{:S(2)}) collective-permute-start(bf16[512,384]{1,0:T(8,128)(2,1)S(1)} %pad_maximum_fusion.17), channel_id=1, source_target_pairs={{0,4},{4,0},{1,5},{5,1},{2,6},{6,2},{3,7},{7,3},{8,12},{12,8},{9,1... | collective-permute-start | bytes 1179656 | tf_op jit(solution)/shard_map/ppermute | solution.py:36
  272.1 3.9 collective-permute-start.48
  275.5 11.5 %collective-permute-start.41 = (bf16[4,96,576]{2,1,0:T(8,128)(2,1)S(1)}, bf16[4,96,576]{2,1,0:T(8,128)(2,1)S(1)}, u32[]{:S(2)}, u32[]{:S(2)}) collective-permute-start(bf16[4,96,576]{2,1,0:T(8,128)(2,1)S(1)} %dynamic-slice_bitcast_fusion.3), channel_id=1, source_target_pairs={{0,4},{4,0},{1,5},{5,1},{2,6},{6,2},{3,7},{7,3},{8,12},{12,8},{9,1... | collective-permute-start | bytes 1327112 | tf_op jit(solution)/shard_map/ppermute | solution.py:36
  276.0 3.9 collective-permute-start.49
  279.9 20.3 %collective-permute-start.37 = (bf16[384,768]{1,0:T(8,128)(2,1)S(1)}, bf16[384,768]{1,0:T(8,128)(2,1)S(1)}, u32[]{:S(2)}, u32[]{:S(2)}) collective-permute-start(bf16[384,768]{1,0:T(8,128)(2,1)S(1)} %get-tuple-element.128), channel_id=1, source_target_pairs={{0,1},{1,0},{2,3},{3,2},{4,5},{5,4},{6,7},{7,6},{8,9},{9,8},{10,11... | collective-permute-start | bytes 1769480 | tf_op jit(solution)/shard_map/ppermute | solution.py:36
  279.9 4.8 %collective-permute-start.50 = (f32[8,768]{1,0:T(8,128)S(1)}, f32[8,768]{1,0:T(8,128)S(1)}, u32[]{:S(2)}, u32[]{:S(2)}) collective-permute-start(f32[8,768]{1,0:T(8,128)S(1)} %add.551), channel_id=1, source_target_pairs={{0,16},{8,24},{16,0},{24,8},{1,17},{9,25},{17,1},{25,9},{2,18},{10... | collective-permute-start | bytes 73736 | tf_op jit(solution)/shard_map/ppermute | solution.py:36
  287.1 7.4 %collective-permute-start.42 = (bf16[96,576]{1,0:T(8,128)(2,1)S(1)}, bf16[96,576]{1,0:T(8,128)(2,1)S(1)}, u32[]{:S(2)}, u32[]{:S(2)}) collective-permute-start(bf16[96,576]{1,0:T(8,128)(2,1)S(1)} %get-tuple-element.152), channel_id=1, source_target_pairs={{0,8},{8,16},{16,24},{24,0},{1,9},{9,17},{17,25},{25,1},{2,10},{10... | collective-permute-start | bytes 331784 | tf_op jit(solution)/shard_map/ppermute | solution.py:41
  288.7 8.6 %collective-permute-start.43 = (bf16[96,576]{1,0:T(8,128)(2,1)S(1)}, bf16[96,576]{1,0:T(8,128)(2,1)S(1)}, u32[]{:S(2)}, u32[]{:S(2)}) collective-permute-start(bf16[96,576]{1,0:T(8,128)(2,1)S(1)} %get-tuple-element.154), channel_id=1, source_target_pairs={{0,16},{8,24},{16,0},{24,8},{1,17},{9,25},{17,1},{25,9},{2,18},{10... | collective-permute-start | bytes 331784 | tf_op jit(solution)/shard_map/ppermute | solution.py:41
  294.5 5.6 %collective-permute-start.44 = (bf16[96,576]{1,0:T(8,128)(2,1)S(1)}, bf16[96,576]{1,0:T(8,128)(2,1)S(1)}, u32[]{:S(2)}, u32[]{:S(2)}) collective-permute-start(bf16[96,576]{1,0:T(8,128)(2,1)S(1)} %get-tuple-element.153), channel_id=1, source_target_pairs={{0,24},{8,0},{16,8},{24,16},{1,25},{9,1},{17,9},{25,17},{2,26},{10... | collective-permute-start | bytes 331784 | tf_op jit(solution)/shard_map/ppermute | solution.py:41
  297.3 20.0 %collective-permute-start.52 = (bf16[384,1728]{0,1:T(8,128)(2,1)S(1)}, bf16[384,1728]{0,1:T(8,128)(2,1)S(1)}, u32[]{:S(2)}, u32[]{:S(2)}) collective-permute-start(bf16[384,1728]{0,1:T(8,128)(2,1)S(1)} %copy-done.23), channel_id=1, source_target_pairs={{0,1},{1,0},{2,3},{3,2},{4,5},{5,4},{6,7},{7,6},{8,9},{9,8},{10,11... | collective-permute-start | bytes 3981320 | tf_op jit(solution)/shard_map/ppermute | solution.py:36
  300.2 58.8 %collective-permute-start.36 = (bf16[384,768]{1,0:T(8,128)(2,1)}, bf16[384,768]{1,0:T(8,128)(2,1)S(1)}, u32[]{:S(2)}, u32[]{:S(2)}) collective-permute-start(bf16[384,768]{1,0:T(8,128)(2,1)} %get-tuple-element.127), channel_id=1, source_target_pairs={{0,1},{1,0},{2,3},{3,2},{4,5},{5,4},{6,7},{7,6},{8,9},{9,8},{10,11... | collective-permute-start | bytes 1769480 | tf_op jit(solution)/shard_map/ppermute | solution.py:36
  300.2 5.8 %collective-permute-start.45 = (bf16[96,576]{1,0:T(8,128)(2,1)S(1)}, bf16[96,576]{1,0:T(8,128)(2,1)S(1)}, u32[]{:S(2)}, u32[]{:S(2)}) collective-permute-start(bf16[96,576]{1,0:T(8,128)(2,1)S(1)} %fusion.104), channel_id=1, source_target_pairs={{0,4},{4,0},{1,5},{5,1},{2,6},{6,2},{3,7},{7,3},{8,12},{12,8},{9,1... | collective-permute-start | bytes 331784 | tf_op jit(solution)/shard_map/ppermute | solution.py:36
  306.0 56.3 %collective-permute-start.31 = (bf16[2,384,768]{2,1,0:T(8,128)(2,1)}, bf16[2,384,768]{2,1,0:T(8,128)(2,1)}, u32[]{:S(2)}, u32[]{:S(2)}) collective-permute-start(bf16[2,384,768]{2,1,0:T(8,128)(2,1)} %pad_maximum_fusion.7), channel_id=1, source_target_pairs={{0,1},{1,0},{2,3},{3,2},{4,5},{5,4},{6,7},{7,6},{8,9},{9,8},{10,11... | collective-permute-start | bytes 3538952 | tf_op jit(solution)/shard_map/ppermute | solution.py:36
  306.1 52.8 %collective-permute-start.38 = (bf16[384,768]{1,0:T(8,128)(2,1)}, bf16[384,768]{1,0:T(8,128)(2,1)}, u32[]{:S(2)}, u32[]{:S(2)}) collective-permute-start(bf16[384,768]{1,0:T(8,128)(2,1)} %bitcast_add_fusion.1), channel_id=1, source_target_pairs={{0,2},{1,3},{2,0},{3,1},{4,6},{5,7},{6,4},{7,5},{8,10},{9,11},{10,... | collective-permute-start | bytes 1769480 | tf_op jit(solution)/shard_map/ppermute | solution.py:36
  314.9 35.8 %collective-permute-start.54 = (bf16[384,1728]{0,1:T(8,128)(2,1)}, bf16[384,1728]{0,1:T(8,128)(2,1)}, u32[]{:S(2)}, u32[]{:S(2)}) collective-permute-start(bf16[384,1728]{0,1:T(8,128)(2,1)} %get-tuple-element.124), channel_id=1, source_target_pairs={{0,2},{1,3},{2,0},{3,1},{4,6},{5,7},{6,4},{7,5},{8,10},{9,11},{10,... | collective-permute-start | bytes 3981320 | tf_op jit(solution)/shard_map/ppermute | solution.py:36
  357.6 33.4 %collective-permute-start.56 = (bf16[2,2,96,1728]{3,2,1,0:T(8,128)(2,1)}, bf16[2,2,96,1728]{3,2,1,0:T(8,128)(2,1)}, u32[]{:S(2)}, u32[]{:S(2)}) collective-permute-start(bf16[2,2,96,1728]{3,2,1,0:T(8,128)(2,1)} %fusion.11), channel_id=1, source_target_pairs={{0,4},{4,0},{1,5},{5,1},{2,6},{6,2},{3,7},{7,3},{8,12},{12,8},{9,1... | collective-permute-start | bytes 3981320 | tf_op jit(solution)/shard_map/ppermute | solution.py:36
  361.8 14.7 %collective-permute-start.39 = (bf16[384,768]{1,0:T(8,128)(2,1)S(1)}, bf16[384,768]{1,0:T(8,128)(2,1)S(1)}, u32[]{:S(2)}, u32[]{:S(2)}) collective-permute-start(bf16[384,768]{1,0:T(8,128)(2,1)S(1)} %get-tuple-element.120), channel_id=1, source_target_pairs={{0,2},{1,3},{2,0},{3,1},{4,6},{5,7},{6,4},{7,5},{8,10},{9,11},{10,... | collective-permute-start | bytes 1769480 | tf_op jit(solution)/shard_map/ppermute | solution.py:36
  377.7 15.6 %collective-permute-start.40 = (bf16[2,384,768]{2,1,0:T(8,128)(2,1)}, bf16[2,384,768]{2,1,0:T(8,128)(2,1)}, u32[]{:S(2)}, u32[]{:S(2)}) collective-permute-start(bf16[2,384,768]{2,1,0:T(8,128)(2,1)} %pad_maximum_fusion.8), channel_id=1, source_target_pairs={{0,1},{1,0},{2,3},{3,2},{4,5},{5,4},{6,7},{7,6},{8,9},{9,8},{10,11... | collective-permute-start | bytes 3538952 | tf_op jit(solution)/shard_map/ppermute | solution.py:36
  381.4 23.0 %collective-permute-start.55 = (bf16[2,96,1728]{2,1,0:T(8,128)(2,1)S(1)}, bf16[2,96,1728]{2,1,0:T(8,128)(2,1)S(1)}, u32[]{:S(2)}, u32[]{:S(2)}) collective-permute-start(bf16[2,96,1728]{2,1,0:T(8,128)(2,1)S(1)} %dynamic-slice_bitcast_fusion), channel_id=1, source_target_pairs={{0,4},{4,0},{1,5},{5,1},{2,6},{6,2},{3,7},{7,3},{8,12},{12,8},{9,1... | collective-permute-start | bytes 1990664 | tf_op jit(solution)/shard_map/ppermute | solution.py:36
  392.7 14.9 %collective-permute-start.57 = (bf16[2,96,1728]{2,1,0:T(8,128)(2,1)S(1)}, bf16[2,96,1728]{2,1,0:T(8,128)(2,1)S(1)}, u32[]{:S(2)}, u32[]{:S(2)}) collective-permute-start(bf16[2,96,1728]{2,1,0:T(8,128)(2,1)S(1)} %slice_bitcast_fusion), channel_id=1, source_target_pairs={{0,2},{1,3},{2,0},{3,1},{4,6},{5,7},{6,4},{7,5},{8,10},{9,11},{10,... | collective-permute-start | bytes 1990664 | tf_op jit(solution)/shard_map/ppermute | solution.py:36
  408.1 24.3 %collective-permute-start.58 = (bf16[96,1728]{1,0:T(8,128)(2,1)S(1)}, bf16[96,1728]{1,0:T(8,128)(2,1)S(1)}, u32[]{:S(2)}, u32[]{:S(2)}) collective-permute-start(bf16[96,1728]{1,0:T(8,128)(2,1)S(1)} %get-tuple-element.132), channel_id=1, source_target_pairs={{0,8},{8,16},{16,24},{24,0},{1,9},{9,17},{17,25},{25,1},{2,10},{10... | collective-permute-start | bytes 995336 | tf_op jit(solution)/shard_map/ppermute | solution.py:41
  410.2 26.2 %collective-permute-start.59 = (bf16[96,1728]{1,0:T(8,128)(2,1)S(1)}, bf16[96,1728]{1,0:T(8,128)(2,1)S(1)}, u32[]{:S(2)}, u32[]{:S(2)}) collective-permute-start(bf16[96,1728]{1,0:T(8,128)(2,1)S(1)} %get-tuple-element.133), channel_id=1, source_target_pairs={{0,16},{8,24},{16,0},{24,8},{1,17},{9,25},{17,1},{25,9},{2,18},{10... | collective-permute-start | bytes 995336 | tf_op jit(solution)/shard_map/ppermute | solution.py:41
  410.7 26.8 %collective-permute-start.60 = (bf16[96,1728]{1,0:T(8,128)(2,1)S(1)}, bf16[96,1728]{1,0:T(8,128)(2,1)S(1)}, u32[]{:S(2)}, u32[]{:S(2)}) collective-permute-start(bf16[96,1728]{1,0:T(8,128)(2,1)S(1)} %get-tuple-element.134), channel_id=1, source_target_pairs={{0,24},{8,0},{16,8},{24,16},{1,25},{9,1},{17,9},{25,17},{2,26},{10... | collective-permute-start | bytes 995336 | tf_op jit(solution)/shard_map/ppermute | solution.py:41
  437.7 10.0 %collective-permute-start.61 = (bf16[96,1728]{1,0:T(8,128)(2,1)S(1)}, bf16[96,1728]{1,0:T(8,128)(2,1)S(1)}, u32[]{:S(2)}, u32[]{:S(2)}) collective-permute-start(bf16[96,1728]{1,0:T(8,128)(2,1)S(1)} %fusion.72), channel_id=1, source_target_pairs={{0,4},{4,0},{1,5},{5,1},{2,6},{6,2},{3,7},{7,3},{8,12},{12,8},{9,1... | collective-permute-start | bytes 995336 | tf_op jit(solution)/shard_map/ppermute | solution.py:36
  (56 other events, 233.2 us)
